TPU v7x, 32 devices: a whole 2x2x4 slice. The times are simulated.
32 devices in a mesh: ctx: 8 (over y, x, core), dp: 4 (over z).
Axes of the slice: x: 2, y: 2, z: 4, core: 2. Of those that a mesh axis runs over, the one named last changes fastest.
Arguments:
- hidden_in: bfloat16 [4, 2048, 2048], P('dp', 'ctx'), may hold values from -6 to 6
- queries: bfloat16 [4, 2048, 2048], P('dp', 'ctx'), may hold values from -1000 to 1000
- norm_gain: bfloat16 [2048], replicated, may hold values from 0.099609375 to 1.8984375
- weight_store: bfloat16 [4, 2048, 512], P('dp', 'ctx'), may hold values from -0.125 to 0.125
- owners: int32 [2], replicated, may hold values from 0 to 3, as said below
- doc_lengths: int32 [4, 4], P('dp'), may hold values from 1 to 1024, 2048 in all within a row
Outputs:
- attended: bfloat16 [4, 2048, 2048], P('dp', 'ctx')
Inputs may be any that keep to these rules, and one draw needn't show every extreme that they name: `owners`: two different data ranks, one of them the last rank 4 - 1; the first owns the key projection, the second the value projection.
All inputs are finite; a program needn't handle non-finite values.
Results may differ from a plain program's by a relative error of at most 0.012.
Values may be sent and summed in bfloat16 or wider, within the bound.
No kernel may reach another device: no remote copies, remote signals or barrier semaphores. Data moves between devices by JAX's collectives and lax.ppermute only.
A program may use at most 64 MiB of HBM per device.

v0:
```python
import jax
import jax.numpy as jnp
from jax import lax
from jax.sharding import PartitionSpec as P

HS = 128
REACH = 4


def from_root(block, axis, owner):
    block = jnp.where(lax.axis_index(axis) == owner, block, jnp.zeros_like(block))
    return lax.psum(block, axis)


def from_behind(x, axis, by):
    size = lax.axis_size(axis)
    pairs = [(i, i + by) for i in range(size) if 0 <= i + by < size]
    return lax.ppermute(x, axis, pairs)


def find_starts(lengths, positions):
    ends = jnp.cumsum(lengths)
    starts = ends - lengths
    below = starts[None, :] <= positions[:, None]
    return jnp.max(jnp.where(below, starts[None, :], 0), axis=1)


def copy_owner(slot_rows, owner):
    return from_root(slot_rows, "dp", owner)


def local(hidden_in, queries, norm_gain, weight_store, owners, doc_lengths):
    tok_rows = hidden_in.shape[1]
    key_width = weight_store.shape[2]
    kv_heads = key_width // HS
    group = queries.shape[2] // key_width
    width_all = (REACH + 1) * tok_rows
    ctx_index = lax.axis_index("ctx")
    xf = hidden_in[0].astype(jnp.float32)
    scaled = (
        xf
        * lax.rsqrt(jnp.mean(xf * xf, axis=-1, keepdims=True) + 1e-05)
        * norm_gain.astype(jnp.float32)
    ).astype(jnp.bfloat16)
    own_slot = weight_store[0]
    key_part = copy_owner(own_slot, owners[0])
    value_part = copy_owner(own_slot, owners[1])
    key_sum = jnp.dot(
        scaled,
        lax.all_gather(key_part, "ctx", axis=0, tiled=True),
        preferred_element_type=jnp.float32,
    )
    value_sum = jnp.dot(
        scaled,
        lax.all_gather(value_part, "ctx", axis=0, tiled=True),
        preferred_element_type=jnp.float32,
    )
    kv_own = jnp.stack([key_sum.astype(jnp.bfloat16), value_sum.astype(jnp.bfloat16)])
    earlier = [from_behind(kv_own, "ctx", back) for back in range(REACH, 0, -1)]
    window = jnp.concatenate(earlier + [kv_own], axis=1)
    q_pos = ctx_index * tok_rows + jnp.arange(tok_rows, dtype=jnp.int32)
    k_pos = (ctx_index - REACH) * tok_rows + jnp.arange(width_all, dtype=jnp.int32)
    q_start = find_starts(doc_lengths[0], q_pos)
    allowed = (k_pos[None, :] >= q_start[:, None]) & (k_pos[None, :] <= q_pos[:, None])
    q_heads = jnp.transpose(queries[0].reshape(tok_rows, kv_heads, group, HS), (1, 2, 0, 3))
    k_heads = jnp.transpose(window[0].reshape(width_all, kv_heads, HS), (1, 0, 2))
    v_heads = jnp.transpose(window[1].reshape(width_all, kv_heads, HS), (1, 0, 2))
    inverse_root = 1.0 / jnp.sqrt(jnp.float32(HS))

    def one_head(args):
        q_one, k_one, v_one = args
        rows = q_one.reshape(group * tok_rows, HS)
        score = jnp.dot(rows, k_one.T, preferred_element_type=jnp.float32)
        score = score.reshape(group, tok_rows, width_all) * inverse_root
        score = jnp.where(allowed[None], score, jnp.float32(-1e30))
        top = jnp.max(score, axis=-1, keepdims=True)
        weight = jnp.exp(score - top)
        total = jnp.sum(weight, axis=-1)
        weight_b = weight.astype(jnp.bfloat16).reshape(group * tok_rows, width_all)
        summed = jnp.dot(weight_b, v_one, preferred_element_type=jnp.float32)
        summed = summed.reshape(group, tok_rows, HS)
        return (summed / total[..., None]).astype(jnp.bfloat16)

    outputs = lax.map(one_head, (q_heads, k_heads, v_heads))
    attended = jnp.transpose(outputs, (2, 0, 1, 3)).reshape(1, tok_rows, kv_heads * group * HS)
    return attended


def solution(mesh):
    return jax.shard_map(
        local,
        mesh=mesh,
        in_specs=(
            P("dp", "ctx", None),
            P("dp", "ctx", None),
            P(),
            P("dp", "ctx", None),
            P(),
            P("dp", None),
        ),
        out_specs=P("dp", "ctx", None),
        check_vma=False,
    )
```

profile of v0, /device:TPU:1, one launch (start us, length us, event | category | flops | bytes accessed | tf_op | source)
XLA Modules:
  0.0 198.7 jit_solution(8778680894563662250)
XLA Ops:
  6.5 1.4 fusion.36
  9.3 1.8 select_bitcast_fusion.1
  11.1 39.7 %all-reduce.3.cloned.1.call-done = (bf16[256,512]{1,0:T(8,128)(2,1)}, bf16[256,512]{1,0:T(8,128)(2,1)}) async-done(((bf16[256,512]{1,0:T(8,128)(2,1)}, bf16[256,512]{1,0:T(8,128)(2,1)}), (bf16[256,512]{1,0:T(8,128)(2,1)}, bf16[256,512]{1,0:T(8,128)(2,1)})) %all-reduce.3.cloned.1.call-update) | async-done | bytes 524304 | tf_op jit(solution)/shard_map/psum | solution.py:12
  53.4 28.6 %all-gather.3.cloned.1.call-done = bf16[2048,512]{1,0:T(8,128)(2,1)} async-done(((bf16[256,512]{1,0:T(8,128)(2,1)}), bf16[2048,512]{1,0:T(8,128)(2,1)}) %all-gather.3.cloned.1.call-update) | async-done | bytes 2097168 | tf_op jit(solution)/shard_map/all_gather | solution.py:50
  82.0 2.3 %fusion.30 = bf16[1,256,512]{2,1,0:T(8,128)(2,1)S(1)} fusion(bf16[2048,512]{1,0:T(8,128)(2,1)} %all-gather.3.cloned.1.call-done, bf16[1,256,2048]{2,1,0:T(8,128)(2,1)S(1)} %copy-done, f32[2048]{0:T(1024)S(1)} %convert_element_type.26, f32[256]{0:T(256)S(1)} %add_rsqrt_fusion), kind=kOutput, calls=%fused_computation.29 | convolution fusion | flops 539099136 | bytes 3417088 | tf_op jit(solution)/shard_map/dot_general | solution.py:48
  84.4 27.5 %all-gather.5.cloned.1.call-done = bf16[2048,512]{1,0:T(8,128)(2,1)} async-done(((bf16[256,512]{1,0:T(8,128)(2,1)}), bf16[2048,512]{1,0:T(8,128)(2,1)}) %all-gather.5.cloned.1.call-update) | async-done | bytes 2097168 | tf_op jit(solution)/shard_map/all_gather | solution.py:55
  111.8 2.3 %fusion.31 = bf16[1,256,512]{2,1,0:T(8,128)(2,1)S(1)} fusion(bf16[2048,512]{1,0:T(8,128)(2,1)} %all-gather.5.cloned.1.call-done, bf16[1,256,2048]{2,1,0:T(8,128)(2,1)S(1)} %copy-done, f32[2048]{0:T(1024)S(1)} %convert_element_type.26, f32[256]{0:T(256)S(1)} %add_rsqrt_fusion), kind=kOutput, calls=%fused_computation.30 | convolution fusion | flops 539099136 | bytes 3417088 | tf_op jit(solution)/shard_map/dot_general | solution.py:53
  115.7 3.8 %collective-permute-start = (bf16[2,256,512]{2,1,0:T(8,128)(2,1)}, bf16[2,256,512]{2,1,0:T(8,128)(2,1)}, u32[]{:S(2)}, u32[]{:S(2)}) collective-permute-start(bf16[2,256,512]{2,1,0:T(8,128)(2,1)} %pad_maximum_fusion), channel_id=1, source_target_pairs={{0,16},{4,20},{8,24},{12,28},{1,17},{5,21},{9,25},{13,29},{2,18},{... | collective-permute-start | bytes 1572872 | tf_op jit(solution)/shard_map/ppermute | solution.py:18
  119.5 2.1 %collective-permute-start.1 = (bf16[2,256,512]{2,1,0:T(8,128)(2,1)}, bf16[2,256,512]{2,1,0:T(8,128)(2,1)}, u32[]{:S(2)}, u32[]{:S(2)}) collective-permute-start(bf16[2,256,512]{2,1,0:T(8,128)(2,1)} %pad_maximum_fusion), channel_id=1, source_target_pairs={{0,12},{4,16},{8,20},{12,24},{16,28},{1,13},{5,17},{9,21},{13,25},... | collective-permute-start | bytes 1572872 | tf_op jit(solution)/shard_map/ppermute | solution.py:18
  121.6 2.9 %collective-permute-start.2 = (bf16[2,256,512]{2,1,0:T(8,128)(2,1)}, bf16[2,256,512]{2,1,0:T(8,128)(2,1)}, u32[]{:S(2)}, u32[]{:S(2)}) collective-permute-start(bf16[2,256,512]{2,1,0:T(8,128)(2,1)} %pad_maximum_fusion), channel_id=1, source_target_pairs={{0,8},{4,12},{8,16},{12,20},{16,24},{20,28},{1,9},{5,13},{9,17},{1... | collective-permute-start | bytes 1572872 | tf_op jit(solution)/shard_map/ppermute | solution.py:18
  124.5 1.9 collective-permute-start.3
  127.1 25.4 %collective-permute-done = bf16[2,256,512]{2,1,0:T(8,128)(2,1)} collective-permute-done((bf16[2,256,512]{2,1,0:T(8,128)(2,1)}, bf16[2,256,512]{2,1,0:T(8,128)(2,1)}, u32[]{:S(2)}, u32[]{:S(2)}) %collective-permute-start) | collective-permute-done | bytes 524320 | tf_op jit(solution)/shard_map/ppermute | solution.py:18
  153.6 5.2 %collective-permute-done.1 = bf16[2,256,512]{2,1,0:T(8,128)(2,1)} collective-permute-done((bf16[2,256,512]{2,1,0:T(8,128)(2,1)}, bf16[2,256,512]{2,1,0:T(8,128)(2,1)}, u32[]{:S(2)}, u32[]{:S(2)}) %collective-permute-start.1) | collective-permute-done | bytes 524320 | tf_op jit(solution)/shard_map/ppermute | solution.py:18
  163.4 3.6 %reshape_squeeze.10 = bf16[1280,4,128]{2,1,0:T(4,128)(2,1)} reshape(bf16[1,1280,512]{2,1,0:T(8,128)(2,1)} %get-tuple-element.96) | data formatting | bytes 2621440 | tf_op jit(solution)/shard_map/reshape;squeeze | solution.py:66
  168.2 3.1 %copy_bitcast_fusion = (bf16[4,1280,128]{2,1,0:T(8,128)(2,1)}, bf16[4,1280,128]{2,1,0:T(8,128)(2,1)S(1)}) fusion(bf16[1280,4,128]{2,1,0:T(4,128)(2,1)} %reshape_squeeze.11, bf16[1280,4,128]{2,1,0:T(4,128)(2,1)} %reshape_squeeze.10), kind=kLoop, calls=%fused_computation.25 | loop fusion | bytes 5242880 | tf_op jit(solution)/shard_map/transpose | solution.py:67
  171.3 18.5 %while.11 = (s32[]{:T(128)}, bf16[4,4,256,128]{3,2,1,0:T(8,128)(2,1)S(1)}, bf16[4,4,256,128]{2,3,1,0:T(8,128)(2,1)S(1)}, bf16[4,1280,128]{2,1,0:T(8,128)(2,1)S(1...) while((s32[]{:T(128)}, ...), condition=%wide.region_8.9_spmd.clone, body=%wide.region_5.8_spmd.clone.sunk | while | flops 681506816 | bytes 17593436 | solution.py:84
  173.9 2.0 %fusion.48 = bf16[4,4,256,128]{3,2,1,0:T(8,128)(2,1)S(1)} fusion(bf16[4,4,256,128]{3,2,1,0:T(8,128)(2,1)S(1)} %get-tuple-element.166, s32[]{:T(128)} %get-tuple-element.165, f32[4,256,1280]{2,1,0:T(8,128)S(1)} %get-tuple-element.154, f32[4,256]{1,0:T(4,128)S(1)} %get-tuple-element.155, bf16[4,1280,128]{2,1,0:T(8,128)(2,1)} %get-tuple-element.178, ...), kind=kOutput, calls=%fused_computation.11.clone.1 | convolution fusion | flops 338427904 | bytes 5841920 | tf_op jit(solution)/shard_map/while/body/eval_jaxpr/dot_general | solution.py:80
  176.2 1.3 fusion.46
  178.5 2.0 %fusion.48 = bf16[4,4,256,128]{3,2,1,0:T(8,128)(2,1)S(1)} fusion(bf16[4,4,256,128]{3,2,1,0:T(8,128)(2,1)S(1)} %get-tuple-element.166, s32[]{:T(128)} %get-tuple-element.165, f32[4,256,1280]{2,1,0:T(8,128)S(1)} %get-tuple-element.154, f32[4,256]{1,0:T(4,128)S(1)} %get-tuple-element.155, bf16[4,1280,128]{2,1,0:T(8,128)(2,1)} %get-tuple-element.178, ...), kind=kOutput, calls=%fused_computation.11.clone.1 | convolution fusion | flops 338427904 | bytes 5841920 | tf_op jit(solution)/shard_map/while/body/eval_jaxpr/dot_general | solution.py:80
  180.8 1.3 fusion.46
  183.1 2.0 %fusion.48 = bf16[4,4,256,128]{3,2,1,0:T(8,128)(2,1)S(1)} fusion(bf16[4,4,256,128]{3,2,1,0:T(8,128)(2,1)S(1)} %get-tuple-element.166, s32[]{:T(128)} %get-tuple-element.165, f32[4,256,1280]{2,1,0:T(8,128)S(1)} %get-tuple-element.154, f32[4,256]{1,0:T(4,128)S(1)} %get-tuple-element.155, bf16[4,1280,128]{2,1,0:T(8,128)(2,1)} %get-tuple-element.178, ...), kind=kOutput, calls=%fused_computation.11.clone.1 | convolution fusion | flops 338427904 | bytes 5841920 | tf_op jit(solution)/shard_map/while/body/eval_jaxpr/dot_general | solution.py:80
  185.5 1.3 fusion.46
  187.7 2.0 %fusion.48 = bf16[4,4,256,128]{3,2,1,0:T(8,128)(2,1)S(1)} fusion(bf16[4,4,256,128]{3,2,1,0:T(8,128)(2,1)S(1)} %get-tuple-element.166, s32[]{:T(128)} %get-tuple-element.165, f32[4,256,1280]{2,1,0:T(8,128)S(1)} %get-tuple-element.154, f32[4,256]{1,0:T(4,128)S(1)} %get-tuple-element.155, bf16[4,1280,128]{2,1,0:T(8,128)(2,1)} %get-tuple-element.178, ...), kind=kOutput, calls=%fused_computation.11.clone.1 | convolution fusion | flops 338427904 | bytes 5841920 | tf_op jit(solution)/shard_map/while/body/eval_jaxpr/dot_general | solution.py:80
  190.6 1.6 reshape.47
  (46 shorter events, 18.9 us)
Async XLA Ops:
  6.5 46.5 %copy-start = (bf16[1,256,2048]{2,1,0:T(8,128)(2,1)S(1)}, bf16[1,256,2048]{2,1,0:T(8,128)(2,1)}, u32[]{:S(2)}) copy-start(bf16[1,256,2048]{2,1,0:T(8,128)(2,1)} %param.8) | copy-start | bytes 3145732
  6.5 44.3 %all-reduce.3.cloned.1.call-start = ((), (), s32[]{:S(2)}) async-start(), calls=%async_computation.2 | async-start | bytes 1048576 | tf_op jit(solution)/shard_map/psum | solution.py:12
  11.1 70.9 %all-gather.3.cloned.1.call-start = ((), (), s32[]{:S(2)}) async-start(), calls=%async_computation | async-start | bytes 2359296 | tf_op jit(solution)/shard_map/all_gather | solution.py:50
  50.8 61.0 %all-gather.5.cloned.1.call-start = ((), (), s32[]{:S(2)}) async-start(), calls=%async_computation.1 | async-start | bytes 2359296 | tf_op jit(solution)/shard_map/all_gather | solution.py:55
  84.3 37.3 %copy-start.4 = (s32[1,4]{1,0:T(1,128)S(1)}, s32[1,4]{1,0:T(1,128)}, u32[]{:S(2)}) copy-start(s32[1,4]{1,0:T(1,128)} %param.13) | copy-start | bytes 52
  84.3 42.1 %copy-start.1 = (bf16[1,256,2048]{2,1,0:T(8,128)(2,1)S(1)}, bf16[1,256,2048]{2,1,0:T(8,128)(2,1)}, u32[]{:S(2)}) copy-start(bf16[1,256,2048]{2,1,0:T(8,128)(2,1)} %param.9) | copy-start | bytes 3145732
  114.2 0.7 copy-start.2
  115.7 36.8 %collective-permute-start = (bf16[2,256,512]{2,1,0:T(8,128)(2,1)}, bf16[2,256,512]{2,1,0:T(8,128)(2,1)}, u32[]{:S(2)}, u32[]{:S(2)}) collective-permute-start(bf16[2,256,512]{2,1,0:T(8,128)(2,1)} %pad_maximum_fusion), channel_id=1, source_target_pairs={{0,16},{4,20},{8,24},{12,28},{1,17},{5,21},{9,25},{13,29},{2,18},{... | collective-permute-start | bytes 1572872 | tf_op jit(solution)/shard_map/ppermute | solution.py:18
  119.5 39.3 %collective-permute-start.1 = (bf16[2,256,512]{2,1,0:T(8,128)(2,1)}, bf16[2,256,512]{2,1,0:T(8,128)(2,1)}, u32[]{:S(2)}, u32[]{:S(2)}) collective-permute-start(bf16[2,256,512]{2,1,0:T(8,128)(2,1)} %pad_maximum_fusion), channel_id=1, source_target_pairs={{0,12},{4,16},{8,20},{12,24},{16,28},{1,13},{5,17},{9,21},{13,25},... | collective-permute-start | bytes 1572872 | tf_op jit(solution)/shard_map/ppermute | solution.py:18
  121.6 38.3 %collective-permute-start.2 = (bf16[2,256,512]{2,1,0:T(8,128)(2,1)}, bf16[2,256,512]{2,1,0:T(8,128)(2,1)}, u32[]{:S(2)}, u32[]{:S(2)}) collective-permute-start(bf16[2,256,512]{2,1,0:T(8,128)(2,1)} %pad_maximum_fusion), channel_id=1, source_target_pairs={{0,8},{4,12},{8,16},{12,20},{16,24},{20,28},{1,9},{5,13},{9,17},{1... | collective-permute-start | bytes 1572872 | tf_op jit(solution)/shard_map/ppermute | solution.py:18
  124.5 36.5 %collective-permute-start.3 = (bf16[2,256,512]{2,1,0:T(8,128)(2,1)}, bf16[2,256,512]{2,1,0:T(8,128)(2,1)}, u32[]{:S(2)}, u32[]{:S(2)}) collective-permute-start(bf16[2,256,512]{2,1,0:T(8,128)(2,1)} %pad_maximum_fusion), channel_id=1, source_target_pairs={{0,4},{4,8},{8,12},{12,16},{16,20},{20,24},{24,28},{1,5},{5,9},{9,... | collective-permute-start | bytes 1572872 | tf_op jit(solution)/shard_map/ppermute | solution.py:18
  127.1 35.0 %copy-start.3 = (bf16[1,256,512]{2,1,0:T(8,128)(2,1)S(1)}, bf16[1,256,512]{2,1,0:T(8,128)(2,1)}, u32[]{:S(2)}) copy-start(bf16[1,256,512]{2,1,0:T(8,128)(2,1)} %copy-done.2) | copy-start | bytes 786436
Sparse Core Ops, SparseCore 0:
  11.2 39.5 all-reduce.2
  52.7 29.2 all-gather.2
  83.9 27.8 all-gather.4
where the time goes:
time: 199 us
  waiting for transfers between devices  127 us (64%)
  local copies, waits for them, and re-layouts  18.5 us (9%)
  matrix products  17.9 us (9%)
  between operations  14.6 us (7%)
  starting transfers between devices  10.8 us (5%)
  other arithmetic  9.72 us (5%)
    psum x1, waiting for transfers between devices, from_root(): return lax.psum(block, axis)  39.7 us
    ppermute x4, waiting for transfers between devices, from_behind(): return lax.ppermute(x, axis, pairs)  30.6 us
    all_gather x1, waiting for transfers between devices, local(): lax.all_gather(key_part, 'ctx', axis=0, tiled=True)  28.6 us
    all_gather x1, waiting for transfers between devices, local(): lax.all_gather(value_part, 'ctx', axis=0, tiled=True)  27.5 us
    ppermute x4, starting transfers between devices, from_behind(): return lax.ppermute(x, axis, pairs)  10.7 us
    dot_general x4, matrix products, one_head(): summed = jnp.dot(weight_b, v_one, preferred_element_type=jnp.float32)  8.07 us
    unnamed x15, local copies, waits for them, and re-layouts  5.55 us
    dot_general x4, matrix products, one_head(): score = jnp.dot(rows, k_one.T, preferred_element_type=jnp.float32)  5.14 us
  transfers between devices with their start and end apart: 7, of which 5 were waited for; matrix products, arithmetic and copies ran while one was open for 4% of the time, Pallas kernels for 0%

commit v1 on v0

v1 whole, which is shorter than its diff:
```python
import functools

import jax
import jax.numpy as jnp
import numpy as np
from jax import lax
from jax.experimental import pallas as pl
from jax.experimental.pallas import tpu as pltpu
from jax.sharding import Mesh
from jax.sharding import PartitionSpec as P

HS = 128
REACH = 4
CORES = 2
SWAP = [(0, 1), (1, 0)]
MASKED = -1e30


def attend_kernel(back, chip_ref, docs_ref, q_ref, *refs):
    kv_refs = refs[: back + 1]
    out_ref, bias_ref = refs[back + 1], refs[back + 2]
    tokens = q_ref.shape[0]
    block = tokens // CORES
    half = kv_refs[0].shape[1] // 2
    heads = half // HS
    group = q_ref.shape[1] // half
    width = (REACH + 1) * block
    factor = 1.4426950408889634 / np.sqrt(HS)
    first_key = (chip_ref[0] - back) * tokens
    for b in range(CORES):
        q_pos = back * tokens + b * block + lax.broadcasted_iota(jnp.int32, (block, 1), 0)
        start = jnp.full((block, 1), -(2**30), jnp.int32)
        prefix = -first_key
        for d in range(docs_ref.shape[0]):
            start = jnp.where(q_pos >= prefix, prefix, start)
            prefix = prefix + docs_ref[d]
        k_pos = b * block + lax.broadcasted_iota(jnp.int32, (block, width), 1)
        allowed = (k_pos >= start) & (k_pos <= q_pos)
        bias_ref[b] = jnp.where(allowed, 0.0, MASKED)

    def window(low, columns):
        parts = []
        for i, ref in enumerate(kv_refs):
            lo, hi = max(low - i * tokens, 0), min(low + width - i * tokens, tokens)
            if lo < hi:
                parts.append(ref[lo:hi, columns])
        return jnp.concatenate(parts, axis=0)

    for h in range(heads):
        for b in range(CORES):
            keys = window(b * block, pl.ds(h * HS, HS))
            values = window(b * block, pl.ds(half + h * HS, HS))
            for g in range(group):
                at = pl.ds((h * group + g) * HS, HS)
                rows = pl.ds(b * block, block)
                score = lax.dot_general(
                    q_ref[rows, at], keys, (((1,), (1,)), ((), ())), preferred_element_type=jnp.float32
                )
                score = score + bias_ref[b]
                top = jnp.max(score, axis=-1, keepdims=True)
                weight = jnp.exp2((score - top) * factor)
                total = jnp.sum(weight, axis=-1, keepdims=True)
                summed = jnp.dot(weight.astype(jnp.bfloat16), values, preferred_element_type=jnp.float32)
                out_ref[rows, at] = (summed / total).astype(jnp.bfloat16)


def attend(chip, docs, q, kvs):
    tokens, block = q.shape[0], q.shape[0] // CORES
    smem = pl.BlockSpec(memory_space=pltpu.SMEM)
    vmem = pl.BlockSpec(memory_space=pltpu.VMEM)
    return pl.pallas_call(
        functools.partial(attend_kernel, len(kvs) - 1),
        out_shape=jax.ShapeDtypeStruct(q.shape, jnp.bfloat16),
        in_specs=[smem, smem, vmem] + [vmem] * len(kvs),
        out_specs=vmem,
        scratch_shapes=[pltpu.VMEM((CORES, block, (REACH + 1) * block), jnp.float32)],
        compiler_params=pltpu.CompilerParams(vmem_limit_bytes=48 << 20),
        name="attend",
    )(chip, docs, q, *kvs)


def both_cores(core, own, other, axis):
    return jnp.where(
        core == 0, jnp.concatenate([own, other], axis), jnp.concatenate([other, own], axis)
    )


def local(n_chip, n_dp, hidden_in, queries, norm_gain, weight_store, owners, doc_lengths):
    core = lax.axis_index("core")
    chip = lax.axis_index("chip")
    rank = lax.axis_index("dp")
    slot = weight_store[0]
    half = slot.shape[1] // CORES
    slot_own = lax.dynamic_slice_in_dim(slot, core * half, half, 1)
    slot_other = lax.dynamic_slice_in_dim(slot, (1 - core) * half, half, 1)
    chunk = both_cores(core, slot_own, lax.ppermute(slot_other, "core", SWAP), 0)
    slots = [chunk] + [
        lax.ppermute(chunk, "dp", [(i, (i + k) % n_dp) for i in range(n_dp)]) for k in range(1, n_dp)
    ]

    xf = hidden_in[0].astype(jnp.float32)
    scaled = (
        xf
        * lax.rsqrt(jnp.mean(xf * xf, axis=-1, keepdims=True) + 1e-05)
        * norm_gain.astype(jnp.float32)
    ).astype(jnp.bfloat16)
    scaled = both_cores(core, scaled, lax.ppermute(scaled, "core", SWAP), 0)
    q_half = queries.shape[2] // CORES
    q_own = lax.dynamic_slice_in_dim(queries[0], core * q_half, q_half, 1)
    q_other = lax.dynamic_slice_in_dim(queries[0], (1 - core) * q_half, q_half, 1)
    q = both_cores(core, q_own, lax.ppermute(q_other, "core", SWAP), 0)

    def owned(owner):
        at = lax.rem(rank - owner + n_dp, n_dp)
        chosen = slots[0]
        for k in range(1, n_dp):
            chosen = jnp.where(at == k, slots[k], chosen)
        return chosen

    weights = jnp.concatenate([owned(owners[0]), owned(owners[1])], axis=1)
    rows = weights.shape[0]
    total = jnp.zeros((scaled.shape[0], weights.shape[1]), jnp.float32)
    for k in range(n_chip):
        part = weights
        if k:
            part = lax.ppermute(weights, "chip", [(i, i ^ k) for i in range(n_chip)])
        columns = lax.dynamic_slice_in_dim(scaled, (chip ^ k) * rows, rows, 1)
        total = total + jnp.dot(columns, part, preferred_element_type=jnp.float32)
    kv = total.astype(jnp.bfloat16)
    back = REACH // CORES
    kvs = [
        lax.ppermute(kv, "chip", [(i, i + by) for i in range(n_chip - by)]) for by in range(back, 0, -1)
    ] + [kv]
    out = attend(chip[None], doc_lengths[0], q, kvs)
    tok = hidden_in.shape[1]
    mine = lax.dynamic_slice_in_dim(out, core * tok, tok, 0)
    theirs = lax.dynamic_slice_in_dim(out, (1 - core) * tok, tok, 0)
    return both_cores(core, mine, lax.ppermute(theirs, "core", SWAP), 1)[None]


def solution(mesh):
    n_ctx, n_dp = mesh.shape["ctx"], mesh.shape["dp"]
    n_chip = n_ctx // CORES
    view = Mesh(mesh.devices.reshape(n_chip, CORES, n_dp), ("chip", "core", "dp"))
    rows = P("dp", ("chip", "core"), None)
    return jax.shard_map(
        functools.partial(local, n_chip, n_dp),
        mesh=view,
        in_specs=(rows, rows, P(), rows, P(), P("dp", None)),
        out_specs=rows,
        check_vma=False,
    )
```

time: 199 us -> 105 us (0.53)
  waiting for transfers between devices: 127 us -> 61.8 us
  matrix products: 17.9 us -> 2.86 us
  local copies, waits for them, and re-layouts: 18.5 us -> 3.88 us
  between operations: 14.6 us -> 1.44 us
  Pallas kernels: 0 us -> 10.2 us
  starting transfers between devices: 10.8 us -> 15.8 us
    all_gather x2 -> x0, waiting for transfers between devices: 56.1 us -> none  [the longest x1 28.6 us: local(): lax.all_gather(key_part, 'ctx', axis=0, tiled=True)]
    psum x1 -> x0, waiting for transfers between devices: 39.7 us -> none  [from_root(): return lax.psum(block, axis)]
    ppermute x4 -> x12, waiting for transfers between devices: 30.6 us -> 61.8 us  [the longest x3 21.1 us: local(): part = lax.ppermute(weights, 'chip', [(i, i ^ k) for i in range(n_chip)])]
    dot_general x10 -> x4, matrix products: 17.9 us -> 2.86 us  [local(): total = total + jnp.dot(columns, part, preferred_element_type=jnp.float32)]
    pallas_call x0 -> x1, Pallas kernels: none -> 10.2 us  [attend(): pl.pallas_call(functools.partial(attend_kernel, len(kvs) - 1), out_shape=...]
    unnamed x15 -> x6, local copies, waits for them, and re-layouts: 5.55 us -> 0.01 us
    ppermute x4 -> x12, starting transfers between devices: 10.7 us -> 15.8 us  [the longest x2 5.51 us: local(): lax.ppermute(kv, 'chip', [(i, i + by) for i in range(n_chip - by)])]
    another operation x2 -> x0, local copies, waits for them, and re-layouts: 4.78 us -> none  [the longest x1 3.56 us: local(): window[0].reshape(width_all, kv_heads, HS)]
  transfers between devices with their start and end apart: 7 -> 12, of which waited for: 5 -> 7; matrix products, arithmetic and copies ran while one was open for 4% -> 12% of each run, Pallas kernels for 0% -> 0%
where the time goes in v1:
time: 105 us
  waiting for transfers between devices  61.8 us (59%)
  starting transfers between devices  15.8 us (15%)
  Pallas kernels  10.2 us (10%)
  other arithmetic  8.48 us (8%)
  local copies, waits for them, and re-layouts  3.88 us (4%)
  matrix products  2.86 us (3%)
  between operations  1.44 us (1%)
    ppermute x3, waiting for transfers between devices, local(): part = lax.ppermute(weights, 'chip', [(i, i ^ k) for i in range(n_chip)])  21.1 us
    ppermute x2, waiting for transfers between devices, local(): lax.ppermute(kv, 'chip', [(i, i + by) for i in range(n_chip - by)])  19.7 us
    ppermute x3, waiting for transfers between devices, local(): lax.ppermute(chunk, 'dp', [(i, (i + k) % n_dp) for i in range(n_dp)])  19.5 us
    pallas_call x1, Pallas kernels, attend(): pl.pallas_call(functools.partial(attend_kernel, len(kvs) - 1), out_shape=...  10.2 us
    ppermute x2, starting transfers between devices, local(): lax.ppermute(kv, 'chip', [(i, i + by) for i in range(n_chip - by)])  5.51 us
    ppermute x3, starting transfers between devices, local(): lax.ppermute(chunk, 'dp', [(i, (i + k) % n_dp) for i in range(n_dp)])  4.85 us
    select_n x4, other arithmetic, both_cores(): jnp.where(core == 0, jnp.concatenate([own, other], axis), jnp.concatenate...  4.13 us
    dot_general x4, matrix products, local(): total = total + jnp.dot(columns, part, preferred_element_type=jnp.float32)  2.86 us
  transfers between devices with their start and end apart: 12, of which 7 were waited for; matrix products, arithmetic and copies ran while one was open for 12% of the time, Pallas kernels for 0%

profile of v1, /device:TPU:1, one launch (start us, length us, event | category | flops | bytes accessed | tf_op | source)
XLA Modules:
  0.0 104.5 jit_solution(6565526295224072185)
XLA Ops:
  0.0 1.1 %dynamic-slice_bitcast_fusion.4 = (bf16[256,256]{1,0:T(8,128)(2,1)S(1)}, bf16[256,256]{1,0:T(8,128)(2,1)S(1)}) fusion(bf16[1,256,512]{2,1,0:T(8,128)(2,1)} %param.9, s32[]{:T(128)S(6)} %select_n.111, s32[]{:T(128)S(6)} %select_n.112), kind=kLoop, calls=%fused_computation.27 | loop fusion | bytes 524296 | tf_op jit(solution)/shard_map/dynamic_slice | solution.py:94
  1.2 0.7 convert_element_type.17
  1.9 1.5 %fusion = f32[256]{0:T(256)S(1)} fusion(bf16[1,256,2048]{2,1,0:T(8,128)(2,1)} %param.6), kind=kLoop, calls=%fused_computation.2 | loop fusion | flops 1572608 | bytes 1049600 | tf_op jit(solution)/shard_map/reduce_sum | solution.py:104
  4.4 4.4 %collective-permute-start.3 = (bf16[512,256]{1,0:T(8,128)(2,1)S(1)}, bf16[512,256]{1,0:T(8,128)(2,1)S(1)}, u32[]{:S(2)}, u32[]{:S(2)}) collective-permute-start(bf16[512,256]{1,0:T(8,128)(2,1)S(1)} %maximum_select_fusion.3), channel_id=1, source_target_pairs={{0,3},{1,0},{2,1},{3,2},{4,7},{5,4},{6,5},{7,6},{8,11},{9,8},{10,9... | collective-permute-start | bytes 786440 | tf_op jit(solution)/shard_map/ppermute | solution.py:98
  11.2 2.9 %collective-permute-done.3 = bf16[512,256]{1,0:T(8,128)(2,1)S(1)} collective-permute-done((bf16[512,256]{1,0:T(8,128)(2,1)S(1)}, bf16[512,256]{1,0:T(8,128)(2,1)S(1)}, u32[]{:S(2)}, u32[]{:S(2)}) %collective-permute-start.3) | collective-permute-done | bytes 262176 | tf_op jit(solution)/shard_map/ppermute | solution.py:98
  14.0 16.7 %collective-permute-done.4 = bf16[512,256]{1,0:T(8,128)(2,1)S(1)} collective-permute-done((bf16[512,256]{1,0:T(8,128)(2,1)S(1)}, bf16[512,256]{1,0:T(8,128)(2,1)S(1)}, u32[]{:S(2)}, u32[]{:S(2)}) %collective-permute-start.4) | collective-permute-done | bytes 262176 | tf_op jit(solution)/shard_map/ppermute | solution.py:98
  30.7 1.0 select_select_fusion.1
  31.7 0.8 pad_maximum_fusion
  32.6 1.2 %collective-permute-start.6 = (bf16[512,512]{1,0:T(8,128)(2,1)}, bf16[512,512]{1,0:T(8,128)(2,1)}, u32[]{:S(2)}, u32[]{:S(2)}) collective-permute-start(bf16[512,512]{1,0:T(8,128)(2,1)} %pad_maximum_fusion), channel_id=1, source_target_pairs={{0,8},{8,0},{16,24},{24,16},{1,9},{9,1},{17,25},{25,17},{2,10},{10... | collective-permute-start | bytes 1572872 | tf_op jit(solution)/shard_map/ppermute | solution.py:126
  33.8 2.1 %dynamic-slice_bitcast_fusion.2 = (bf16[256,1024]{1,0:T(8,128)(2,1)S(1)}, bf16[256,1024]{1,0:T(8,128)(2,1)}) fusion(bf16[1,256,2048]{2,1,0:T(8,128)(2,1)} %param.7, s32[]{:T(128)S(6)} %select_n.103, s32[]{:T(128)S(6)} %select_n.104), kind=kLoop, calls=%fused_computation.22 | loop fusion | bytes 2097160 | tf_op jit(solution)/shard_map/dynamic_slice | solution.py:109
  35.8 1.6 %collective-permute-start = (bf16[256,1024]{1,0:T(8,128)(2,1)}, bf16[256,1024]{1,0:T(8,128)(2,1)}, u32[]{:S(2)}, u32[]{:S(2)}) collective-permute-start(bf16[256,1024]{1,0:T(8,128)(2,1)} %get-tuple-element.10), channel_id=1, source_target_pairs={{0,4},{4,0},{1,5},{5,1},{2,6},{6,2},{3,7},{7,3},{8,12},{12,8},{9,1... | collective-permute-start | bytes 1572872 | tf_op jit(solution)/shard_map/ppermute | solution.py:111
  37.4 1.2 %collective-permute-start.7 = (bf16[512,512]{1,0:T(8,128)(2,1)}, bf16[512,512]{1,0:T(8,128)(2,1)S(1)}, u32[]{:S(2)}, u32[]{:S(2)}) collective-permute-start(bf16[512,512]{1,0:T(8,128)(2,1)} %pad_maximum_fusion), channel_id=1, source_target_pairs={{0,16},{8,24},{16,0},{24,8},{1,17},{9,25},{17,1},{25,9},{2,18},{10... | collective-permute-start | bytes 1572872 | tf_op jit(solution)/shard_map/ppermute | solution.py:126
  38.9 1.0 maximum_select_fusion
  39.8 5.1 %collective-permute-done.6 = bf16[512,512]{1,0:T(8,128)(2,1)} collective-permute-done((bf16[512,512]{1,0:T(8,128)(2,1)}, bf16[512,512]{1,0:T(8,128)(2,1)}, u32[]{:S(2)}, u32[]{:S(2)}) %collective-permute-start.6) | collective-permute-done | bytes 524320 | tf_op jit(solution)/shard_map/ppermute | solution.py:126
  45.0 1.5 %fusion.10 = f32[512,512]{1,0:T(8,128)S(1)} fusion(bf16[512,512]{1,0:T(8,128)(2,1)} %collective-permute-done.6, bf16[512,2048]{1,0:T(8,128)(2,1)S(1)} %maximum_select_fusion, s32[]{:T(128)S(6)} %select_n.125), kind=kOutput, calls=%fused_computation.18 | convolution fusion | flops 268435456 | bytes 2097156 | tf_op jit(solution)/shard_map/dot_general | solution.py:128
  46.4 16.0 %collective-permute-done.7 = bf16[512,512]{1,0:T(8,128)(2,1)S(1)} collective-permute-done((bf16[512,512]{1,0:T(8,128)(2,1)}, bf16[512,512]{1,0:T(8,128)(2,1)S(1)}, u32[]{:S(2)}, u32[]{:S(2)}) %collective-permute-start.7) | collective-permute-done | bytes 524320 | tf_op jit(solution)/shard_map/ppermute | solution.py:126
  63.8 2.2 %collective-permute-start.10 = (bf16[512,512]{1,0:T(8,128)(2,1)S(1)}, bf16[512,512]{1,0:T(8,128)(2,1)S(1)}, u32[]{:S(2)}, u32[]{:S(2)}) collective-permute-start(bf16[512,512]{1,0:T(8,128)(2,1)S(1)} %fusion.5.refs_2_), channel_id=1, source_target_pairs={{0,8},{8,16},{16,24},{1,9},{9,17},{17,25},{2,10},{10,18},{18,26},{... | collective-permute-start | bytes 1572872 | tf_op jit(solution)/shard_map/ppermute | solution.py:132
  66.0 3.3 %collective-permute-start.9 = (bf16[512,512]{1,0:T(8,128)(2,1)S(1)}, bf16[512,512]{1,0:T(8,128)(2,1)S(1)}, u32[]{:S(2)}, u32[]{:S(2)}) collective-permute-start(bf16[512,512]{1,0:T(8,128)(2,1)S(1)} %fusion.5.refs_2_), channel_id=1, source_target_pairs={{0,16},{8,24},{1,17},{9,25},{2,18},{10,26},{3,19},{11,27},{4,20},{... | collective-permute-start | bytes 1572872 | tf_op jit(solution)/shard_map/ppermute | solution.py:132
  69.4 1.7 %maximum_select_fusion.1.q_ref = bf16[512,1024]{1,0:T(8,128)(2,1)S(1)} fusion(bf16[256,1024]{1,0:T(8,128)(2,1)} %collective-permute-done, bf16[256,1024]{1,0:T(8,128)(2,1)S(1)} %get-tuple-element.9, pred[]{:T(512)S(6)} %eq.24), kind=kLoop, calls=%fused_computation.10 | loop fusion | flops 4718592 | bytes 2097153 | tf_op jit(solution)/shard_map/jit(_where)/select_n | solution.py:83
  71.1 5.4 %collective-permute-done.10.refs_1_ = bf16[512,512]{1,0:T(8,128)(2,1)S(1)} collective-permute-done((bf16[512,512]{1,0:T(8,128)(2,1)S(1)}, bf16[512,512]{1,0:T(8,128)(2,1)S(1)}, u32[]{:S(2)}, u32[]{:S(2)}) %collective-permute-start.10) | collective-permute-done | bytes 524320 | tf_op jit(solution)/shard_map/ppermute | solution.py:132
  76.4 14.3 %collective-permute-done.9.refs_0_ = bf16[512,512]{1,0:T(8,128)(2,1)S(1)} collective-permute-done((bf16[512,512]{1,0:T(8,128)(2,1)S(1)}, bf16[512,512]{1,0:T(8,128)(2,1)S(1)}, u32[]{:S(2)}, u32[]{:S(2)}) %collective-permute-start.9) | collective-permute-done | bytes 524320 | tf_op jit(solution)/shard_map/ppermute | solution.py:132
  90.8 10.2 %attend.1 = bf16[512,1024]{1,0:T(8,128)(2,1)S(1)} custom-call(s32[1]{0:T(128)} %bitcast.chip_ref, s32[4]{0:T(128)S(1)} %bitcast.22, bf16[512,1024]{1,0:T(8,128)(2,1)S(1)} %maximum_select_fusion.1.q_ref, bf16[512,512]{1,0:T(8,128)(2,1)S(1)} %collective-permute-done.9.refs_0_, bf16[512,512]{1,0:T(8,128)(2,1)S(1)} %collective-permute-done.10.refs_1_, ...), custom_call_target="tpu_custom_call" | custom-call | tf_op jit(solution)/shard_map/attend/pallas_call | solution.py:71
  101.6 1.5 %collective-permute-done.11 = bf16[256,1024]{1,0:T(8,128)(2,1)S(1)} collective-permute-done((bf16[256,1024]{1,0:T(8,128)(2,1)S(1)}, bf16[256,1024]{1,0:T(8,128)(2,1)S(1)}, u32[]{:S(2)}, u32[]{:S(2)}) %collective-permute-start.11) | collective-permute-done | bytes 524320 | tf_op jit(solution)/shard_map/ppermute | solution.py:138
  103.2 1.4 %maximum_select_fusion.2 = bf16[1,256,2048]{2,1,0:T(8,128)(2,1)} fusion(bf16[1,256,1024]{2,1,0:T(8,128)(2,1)S(1)} %bitcast.23, bf16[1,256,1024]{2,1,0:T(8,128)(2,1)S(1)} %get-tuple-element.5, pred[]{:T(512)S(6)} %eq.24), kind=kLoop, calls=%fused_computation.11 | loop fusion | flops 4718592 | bytes 2097153 | tf_op jit(solution)/shard_map/jit(_where)/select_n | solution.py:83
  (25 shorter events, 4.4 us)
Async XLA Ops:
  0.0 3.4 %copy-start.1 = (bf16[1,256,2048]{2,1,0:T(8,128)(2,1)S(1)}, bf16[1,256,2048]{2,1,0:T(8,128)(2,1)}, u32[]{:S(2)}) copy-start(bf16[1,256,2048]{2,1,0:T(8,128)(2,1)} %param.6) | copy-start | bytes 3145732
  0.0 9.2 %copy-start.2 = (s32[2]{0:T(128)S(1)}, s32[2]{0:T(128)}, u32[]{:S(2)}) copy-start(s32[2]{0:T(128)} %param.10) | copy-start | bytes 28
  1.1 3.2 %collective-permute-start.2 = (bf16[256,256]{1,0:T(8,128)(2,1)S(1)}, bf16[256,256]{1,0:T(8,128)(2,1)S(1)}, u32[]{:S(2)}, u32[]{:S(2)}) collective-permute-start(bf16[256,256]{1,0:T(8,128)(2,1)S(1)} %get-tuple-element.12), channel_id=1, source_target_pairs={{0,4},{4,0},{1,5},{5,1},{2,6},{6,2},{3,7},{7,3},{8,12},{12,8},{9,1... | collective-permute-start | bytes 393224 | tf_op jit(solution)/shard_map/ppermute | solution.py:96
  3.7 35.1 %collective-permute-start.1 = (bf16[256,2048]{1,0:T(8,128)(2,1)S(1)}, bf16[256,2048]{1,0:T(8,128)(2,1)S(1)}, u32[]{:S(2)}, u32[]{:S(2)}) collective-permute-start(bf16[256,2048]{1,0:T(8,128)(2,1)S(1)} %fusion.2), channel_id=1, source_target_pairs={{0,4},{4,0},{1,5},{5,1},{2,6},{6,2},{3,7},{7,3},{8,12},{12,8},{9,1... | collective-permute-start | bytes 3145736 | tf_op jit(solution)/shard_map/ppermute | solution.py:107
  4.4 9.7 %collective-permute-start.3 = (bf16[512,256]{1,0:T(8,128)(2,1)S(1)}, bf16[512,256]{1,0:T(8,128)(2,1)S(1)}, u32[]{:S(2)}, u32[]{:S(2)}) collective-permute-start(bf16[512,256]{1,0:T(8,128)(2,1)S(1)} %maximum_select_fusion.3), channel_id=1, source_target_pairs={{0,3},{1,0},{2,1},{3,2},{4,7},{5,4},{6,5},{7,6},{8,11},{9,8},{10,9... | collective-permute-start | bytes 786440 | tf_op jit(solution)/shard_map/ppermute | solution.py:98
  8.8 21.9 %collective-permute-start.4 = (bf16[512,256]{1,0:T(8,128)(2,1)S(1)}, bf16[512,256]{1,0:T(8,128)(2,1)S(1)}, u32[]{:S(2)}, u32[]{:S(2)}) collective-permute-start(bf16[512,256]{1,0:T(8,128)(2,1)S(1)} %maximum_select_fusion.3), channel_id=1, source_target_pairs={{0,2},{1,3},{2,0},{3,1},{4,6},{5,7},{6,4},{7,5},{8,10},{9,11},{10,... | collective-permute-start | bytes 786440 | tf_op jit(solution)/shard_map/ppermute | solution.py:98
  8.8 21.9 %collective-permute-start.5 = (bf16[512,256]{1,0:T(8,128)(2,1)S(1)}, bf16[512,256]{1,0:T(8,128)(2,1)}, u32[]{:S(2)}, u32[]{:S(2)}) collective-permute-start(bf16[512,256]{1,0:T(8,128)(2,1)S(1)} %maximum_select_fusion.3), channel_id=1, source_target_pairs={{0,1},{1,2},{2,3},{3,0},{4,5},{5,6},{6,7},{7,4},{8,9},{9,10},{10,1... | collective-permute-start | bytes 786440 | tf_op jit(solution)/shard_map/ppermute | solution.py:98
  32.6 12.4 %collective-permute-start.6 = (bf16[512,512]{1,0:T(8,128)(2,1)}, bf16[512,512]{1,0:T(8,128)(2,1)}, u32[]{:S(2)}, u32[]{:S(2)}) collective-permute-start(bf16[512,512]{1,0:T(8,128)(2,1)} %pad_maximum_fusion), channel_id=1, source_target_pairs={{0,8},{8,0},{16,24},{24,16},{1,9},{9,1},{17,25},{25,17},{2,10},{10... | collective-permute-start | bytes 1572872 | tf_op jit(solution)/shard_map/ppermute | solution.py:126
  35.8 33.5 %collective-permute-start = (bf16[256,1024]{1,0:T(8,128)(2,1)}, bf16[256,1024]{1,0:T(8,128)(2,1)}, u32[]{:S(2)}, u32[]{:S(2)}) collective-permute-start(bf16[256,1024]{1,0:T(8,128)(2,1)} %get-tuple-element.10), channel_id=1, source_target_pairs={{0,4},{4,0},{1,5},{5,1},{2,6},{6,2},{3,7},{7,3},{8,12},{12,8},{9,1... | collective-permute-start | bytes 1572872 | tf_op jit(solution)/shard_map/ppermute | solution.py:111
  37.4 25.0 %collective-permute-start.7 = (bf16[512,512]{1,0:T(8,128)(2,1)}, bf16[512,512]{1,0:T(8,128)(2,1)S(1)}, u32[]{:S(2)}, u32[]{:S(2)}) collective-permute-start(bf16[512,512]{1,0:T(8,128)(2,1)} %pad_maximum_fusion), channel_id=1, source_target_pairs={{0,16},{8,24},{16,0},{24,8},{1,17},{9,25},{17,1},{25,9},{2,18},{10... | collective-permute-start | bytes 1572872 | tf_op jit(solution)/shard_map/ppermute | solution.py:126
  38.7 24.2 %collective-permute-start.8 = (bf16[512,512]{1,0:T(8,128)(2,1)}, bf16[512,512]{1,0:T(8,128)(2,1)S(1)}, u32[]{:S(2)}, u32[]{:S(2)}) collective-permute-start(bf16[512,512]{1,0:T(8,128)(2,1)} %pad_maximum_fusion), channel_id=1, source_target_pairs={{0,24},{8,16},{16,8},{24,0},{1,25},{9,17},{17,9},{25,1},{2,26},{10... | collective-permute-start | bytes 1572872 | tf_op jit(solution)/shard_map/ppermute | solution.py:126
  63.8 26.9 %copy-start = (s32[1,4]{1,0:T(1,128)S(1)}, s32[1,4]{1,0:T(1,128)}, u32[]{:S(2)}) copy-start(s32[1,4]{1,0:T(1,128)} %param.11) | copy-start | bytes 52
  63.8 12.6 %collective-permute-start.10 = (bf16[512,512]{1,0:T(8,128)(2,1)S(1)}, bf16[512,512]{1,0:T(8,128)(2,1)S(1)}, u32[]{:S(2)}, u32[]{:S(2)}) collective-permute-start(bf16[512,512]{1,0:T(8,128)(2,1)S(1)} %fusion.5.refs_2_), channel_id=1, source_target_pairs={{0,8},{8,16},{16,24},{1,9},{9,17},{17,25},{2,10},{10,18},{18,26},{... | collective-permute-start | bytes 1572872 | tf_op jit(solution)/shard_map/ppermute | solution.py:132
  66.0 24.7 %collective-permute-start.9 = (bf16[512,512]{1,0:T(8,128)(2,1)S(1)}, bf16[512,512]{1,0:T(8,128)(2,1)S(1)}, u32[]{:S(2)}, u32[]{:S(2)}) collective-permute-start(bf16[512,512]{1,0:T(8,128)(2,1)S(1)} %fusion.5.refs_2_), channel_id=1, source_target_pairs={{0,16},{8,24},{1,17},{9,25},{2,18},{10,26},{3,19},{11,27},{4,20},{... | collective-permute-start | bytes 1572872 | tf_op jit(solution)/shard_map/ppermute | solution.py:132
  101.1 2.1 %collective-permute-start.11 = (bf16[256,1024]{1,0:T(8,128)(2,1)S(1)}, bf16[256,1024]{1,0:T(8,128)(2,1)S(1)}, u32[]{:S(2)}, u32[]{:S(2)}) collective-permute-start(bf16[256,1024]{1,0:T(8,128)(2,1)S(1)} %get-tuple-element.6), channel_id=1, source_target_pairs={{0,4},{4,0},{1,5},{5,1},{2,6},{6,2},{3,7},{7,3},{8,12},{12,8},{9,1... | collective-permute-start | bytes 1572872 | tf_op jit(solution)/shard_map/ppermute | solution.py:138

commit v2 on v1

v2 whole, which is shorter than its diff:
```python
import functools

import jax
import jax.numpy as jnp
import numpy as np
from jax import lax
from jax.experimental import pallas as pl
from jax.experimental.pallas import tpu as pltpu
from jax.sharding import PartitionSpec as P

HS = 128
REACH = 4
CORES = 2
MASKED = -1e30
SMEM = pl.BlockSpec(memory_space=pltpu.SMEM)
VMEM = pl.BlockSpec(memory_space=pltpu.VMEM)


def cost(flops):
    return pl.CostEstimate(flops=int(flops), bytes_accessed=1 << 20, transcendentals=0)


def attend_kernel(head, at_ref, docs_ref, own_ref, other_ref, *refs):
    kv_refs, out_ref, bias_ref = refs[:-2], refs[-2], refs[-1]
    core = lax.rem(at_ref[0], CORES)
    block = own_ref.shape[0]
    tokens = kv_refs[0].shape[0]
    back = len(kv_refs) - 1
    group = out_ref.shape[2] // HS
    width = (REACH + 1) * block
    factor = 1.4426950408889634 / np.sqrt(HS)
    first_key = (at_ref[0] // CORES - back) * tokens
    for b in range(CORES):
        q_pos = back * tokens + b * block + lax.broadcasted_iota(jnp.int32, (block, 1), 0)
        start = jnp.full((block, 1), -(2**30), jnp.int32)
        prefix = -first_key
        for d in range(docs_ref.shape[0]):
            start = jnp.where(q_pos >= prefix, prefix, start)
            prefix = prefix + docs_ref[d]
        k_pos = b * block + lax.broadcasted_iota(jnp.int32, (block, width), 1)
        bias_ref[b] = jnp.where((k_pos >= start) & (k_pos <= q_pos), 0.0, MASKED)

    def window(low, columns):
        parts = []
        for i, ref in enumerate(kv_refs):
            lo, hi = max(low - i * tokens, 0), min(low + width - i * tokens, tokens)
            if lo < hi:
                parts.append(ref[lo:hi, columns])
        return jnp.concatenate(parts, axis=0)

    for b in range(CORES):
        keys = window(b * block, pl.ds(0, HS))
        values = window(b * block, pl.ds(HS, HS))
        for g in range(group):
            own = own_ref[:, pl.ds(pl.multiple_of(((head * CORES + core) * group + g) * HS, HS), HS)]
            column = (head * group + g) * HS
            query = jnp.where(core == b, own, other_ref[:, column : column + HS])
            score = lax.dot_general(query, keys, (((1,), (1,)), ((), ())), preferred_element_type=jnp.float32)
            score = score + bias_ref[b]
            top = jnp.max(score, axis=-1, keepdims=True)
            weight = jnp.exp2((score - top) * factor)
            total = jnp.sum(weight, axis=-1, keepdims=True)
            summed = jnp.dot(weight.astype(jnp.bfloat16), values, preferred_element_type=jnp.float32)
            out_ref[core ^ b, :, g * HS : (g + 1) * HS] = (summed / total).astype(jnp.bfloat16)


def attend(head, heads, at, docs, own, other, kvs):
    block = own.shape[0]
    return pl.pallas_call(
        functools.partial(attend_kernel, head),
        out_shape=jax.ShapeDtypeStruct((CORES, own.shape[0], other.shape[1] // heads), jnp.bfloat16),
        in_specs=[SMEM] * 2 + [VMEM] * (2 + len(kvs)),
        out_specs=VMEM,
        scratch_shapes=[pltpu.VMEM((CORES, block, (REACH + 1) * block), jnp.float32)],
        compiler_params=pltpu.CompilerParams(vmem_limit_bytes=32 << 20),
        cost_estimate=cost(5e9),
        name="attend",
    )(at, docs, own, other, *kvs)


def both_cores(core, own, other, axis):
    return jnp.where(
        core == 0, jnp.concatenate([own, other], axis), jnp.concatenate([other, own], axis)
    )


def exchange(x, bit, size, name):
    with jax.named_scope(name):
        return lax.ppermute(x, "ctx", [(i, i ^ bit) for i in range(size)])


def after(x, *others):
    return lax.optimization_barrier((x, others))[0]


def local(n_ctx, n_dp, hidden_in, queries, norm_gain, weight_store, owners, doc_lengths):
    at = lax.axis_index("ctx")
    core = at % CORES
    rank = lax.axis_index("dp")
    slot = weight_store[0]
    rows = slot.shape[0]
    heads = slot.shape[1] // (CORES * HS)
    chips = n_ctx // CORES
    back = REACH // CORES

    pieces = [slot[:, h * CORES * HS : (h + 1) * CORES * HS] for h in range(heads)]

    def over_dp(h, piece):
        slots = [piece]
        for k in range(1, n_dp):
            with jax.named_scope(f"z{h}_{k}"):
                slots.append(lax.ppermute(piece, "dp", [(i, i ^ k) for i in range(n_dp)]))
        return slots

    def owned(slots, owner):
        chosen = slots[0]
        for k in range(1, n_dp):
            chosen = jnp.where((rank ^ owner) == k, slots[k], chosen)
        return chosen

    def forward(x, by, name):
        with jax.named_scope(name):
            return lax.ppermute(x, "ctx", [(i, i + by * CORES) for i in range(n_ctx - by * CORES)])

    slots = over_dp(0, pieces[0])
    xf = hidden_in[0].astype(jnp.float32)
    scaled = (
        xf
        * lax.rsqrt(jnp.mean(xf * xf, axis=-1, keepdims=True) + 1e-05)
        * norm_gain.astype(jnp.float32)
    ).astype(jnp.bfloat16)
    scaled = both_cores(core, scaled, exchange(scaled, 1, n_ctx, "s"), 0)
    columns = [
        jnp.concatenate(
            [lax.dynamic_slice_in_dim(scaled, (at ^ (o * CORES) ^ c) * rows, rows, 1) for c in range(CORES)], axis=1
        )
        for o in range(chips)
    ]
    share = queries.shape[2] // (heads * CORES)
    q_other = jnp.concatenate(
        [lax.dynamic_slice_in_dim(queries[0], (h * CORES + 1 - core) * share, share, 1) for h in range(heads)], axis=1
    )
    q_other = exchange(q_other, 1, n_ctx, "q")

    bits = [CORES << i for i in reversed(range(chips.bit_length() - 1))]
    window = []
    for h in range(heads):
        key, value = owned(slots, owners[0]), owned(slots, owners[1])
        low = jnp.concatenate([key[:, :HS], value[:, :HS]], axis=1)
        high = jnp.concatenate([key[:, HS:], value[:, HS:]], axis=1)
        mine, theirs = jnp.where(core == 0, low, high), jnp.where(core == 0, high, low)
        if h + 1 < heads:
            piece, theirs = lax.optimization_barrier((pieces[h + 1], theirs))
            slots = over_dp(h + 1, piece)
        parts, order = [jnp.concatenate([mine, exchange(theirs, 1, n_ctx, f"c{h}")], axis=0)], [0]
        if h == 0:
            for o in range(CORES, n_ctx, CORES):
                parts.append(exchange(parts[0], o, n_ctx, f"w{h}_{o}"))
                order.append(o)
            slots, columns = lax.optimization_barrier((slots, columns))
        else:
            for bit in bits:
                for i, (o, p) in enumerate(zip(list(order), list(parts))):
                    if i:
                        p = after(p, parts[-1])
                    parts.append(exchange(p, bit, n_ctx, f"w{h}_{bit}_{i}"))
                    order.append(o ^ bit)
        total = None
        for o, part in zip(order, parts):
            product = jnp.dot(columns[o // CORES], part, preferred_element_type=jnp.float32)
            total = product if total is None else total + product
        kv = total.astype(jnp.bfloat16)
        window.append([forward(kv, by, f"kv{h}_{by}") for by in range(back, 0, -1)] + [kv])
    outs = []
    for h in range(heads):
        own = queries[0]
        if h + 1 < heads:
            own = after(own, window[h + 1][-1])
        out = attend(h, heads, at[None], doc_lengths[0], own, q_other, window[h])
        outs.append(both_cores(core, out[0], exchange(out[1], 1, n_ctx, f"o{h}"), 1))
    return jnp.concatenate(outs, axis=1)[None]


def solution(mesh):
    rows = P("dp", "ctx", None)
    return jax.shard_map(
        functools.partial(local, mesh.shape["ctx"], mesh.shape["dp"]),
        mesh=mesh,
        in_specs=(rows, rows, P(), rows, P(), P("dp", None)),
        out_specs=rows,
        check_vma=False,
    )
```

time: 105 us -> 80 us (0.76)
  waiting for transfers between devices: 61.8 us -> 16.5 us
  starting transfers between devices: 15.8 us -> 36.8 us
  local copies, waits for them, and re-layouts: 3.88 us -> 2.12 us
  Pallas kernels: 10.2 us -> 11.4 us
    ppermute x12 -> x22, waiting for transfers between devices: 61.8 us -> 16.5 us  [the longest x12 11.2 us: exchange(): return lax.ppermute(x, 'ctx', [(i, i ^ bit) for i in range(size)])]
    ppermute x12 -> x22, starting transfers between devices: 15.8 us -> 36.8 us  [the longest x12 17.9 us: exchange(): return lax.ppermute(x, 'ctx', [(i, i ^ bit) for i in range(size)])]
    dynamic_slice x2, local copies, waits for them, and re-layouts: 3.13 us -> 0.33 us  [the longest x1 0.29 us: local(): lax.dynamic_slice_in_dim(scaled, (at ^ o * CORES ^ c) * rows, rows, 1)]
    select_n x4 -> x3, other arithmetic: 4.13 us -> 2.66 us  [both_cores(): jnp.where(core == 0, jnp.concatenate([own, other], axis), jnp.concatenate...]
    convert_element_type x1, other arithmetic: 0.31 us -> 1.62 us  [local(): scaled = (xf * lax.rsqrt(jnp.mean(xf * xf, axis=-1, keepdims=True) + 1e-0...]
    pallas_call x1 -> x2, Pallas kernels: 10.2 us -> 11.4 us  [attend(): pl.pallas_call(functools.partial(attend_kernel, head), out_shape=jax.Shap...]
    broadcast_in_dim x0 -> x1, other arithmetic: none -> 1.06 us  [local(): return jnp.concatenate(outs, axis=1)[None]]
    dot_general x4 -> x8, matrix products: 2.86 us -> 2.39 us  [local(): jnp.dot(columns[o // CORES], part, preferred_element_type=jnp.float32)]
  transfers between devices with their start and end apart: 12 -> 22, of which waited for: 7 -> 5; matrix products, arithmetic and copies ran while one was open for 12% -> 14% of each run, Pallas kernels for 0% -> 14%
where the time goes in v2:
time: 80 us; the launch traced here: 79.5 us
  starting transfers between devices  36.8 us (46%)
  waiting for transfers between devices  16.5 us (21%)
  Pallas kernels  11.4 us (14%)
  other arithmetic  8.65 us (11%)
  matrix products  2.39 us (3%)
  local copies, waits for them, and re-layouts  2.12 us (3%)
  between operations  1.76 us (2%)
    ppermute x12, starting transfers between devices, exchange(): return lax.ppermute(x, 'ctx', [(i, i ^ bit) for i in range(size)])  17.9 us
    pallas_call x2, Pallas kernels, attend(): pl.pallas_call(functools.partial(attend_kernel, head), out_shape=jax.Shap...  11.4 us
    ppermute x12, waiting for transfers between devices, exchange(): return lax.ppermute(x, 'ctx', [(i, i ^ bit) for i in range(size)])  11.2 us
    ppermute x4, starting transfers between devices, forward(): lax.ppermute(x, 'ctx', [(i, i + by * CORES) for i in range(n_ctx - by * C...  10.8 us
    ppermute x6, starting transfers between devices, over_dp(): slots.append(lax.ppermute(piece, 'dp', [(i, i ^ k) for i in range(n_dp)]))  8.18 us
    ppermute x6, waiting for transfers between devices, over_dp(): slots.append(lax.ppermute(piece, 'dp', [(i, i ^ k) for i in range(n_dp)]))  5.26 us
    select_n x3, other arithmetic, both_cores(): jnp.where(core == 0, jnp.concatenate([own, other], axis), jnp.concatenate...  2.66 us
    dot_general x8, matrix products, local(): jnp.dot(columns[o // CORES], part, preferred_element_type=jnp.float32)  2.39 us
  transfers between devices with their start and end apart: 22, of which 5 were waited for; matrix products, arithmetic and copies ran while one was open for 14% of the time, Pallas kernels for 14%

profile of v2, /device:TPU:1, one launch (start us, length us, event | category | flops | bytes accessed | tf_op | source)
XLA Modules:
  0.0 79.5 jit_solution(14017095152539887447)
XLA Ops:
  1.0 4.2 %collective-permute-start = (bf16[256,256]{1,0:T(8,128)(2,1)S(1)}, bf16[256,256]{1,0:T(8,128)(2,1)S(1)}, u32[]{:S(2)}, u32[]{:S(2)}) collective-permute-start(bf16[256,256]{1,0:T(8,128)(2,1)S(1)} %slice.67), channel_id=1, source_target_pairs={{0,3},{1,2},{2,1},{3,0},{4,7},{5,6},{6,5},{7,4},{8,11},{9,10},{10,... | collective-permute-start | bytes 393224 | tf_op jit(solution)/shard_map/z0_3/ppermute | solution.py:112
  6.3 1.5 %fusion = f32[256]{0:T(256)S(1)} fusion(bf16[1,256,2048]{2,1,0:T(8,128)(2,1)} %param.6), kind=kLoop, calls=%fused_computation.2 | loop fusion | flops 1572608 | bytes 1049600 | tf_op jit(solution)/shard_map/reduce_sum | solution.py:129
  7.8 1.6 %fusion.2 = bf16[256,2048]{1,0:T(8,128)(2,1)S(1)} fusion(bf16[1,256,2048]{2,1,0:T(8,128)(2,1)} %param.6, f32[2048]{0:T(1024)S(1)} %convert_element_type.20, f32[256]{0:T(256)S(1)} %add_rsqrt_fusion), kind=kLoop, calls=%fused_computation.4 | loop fusion | flops 2097152 | bytes 2106368 | tf_op jit(solution)/shard_map/convert_element_type | solution.py:131
  9.4 1.3 %collective-permute-start.6 = (bf16[256,2048]{1,0:T(8,128)(2,1)S(1)}, bf16[256,2048]{1,0:T(8,128)(2,1)}, u32[]{:S(2)}, u32[]{:S(2)}) collective-permute-start(bf16[256,2048]{1,0:T(8,128)(2,1)S(1)} %fusion.2), channel_id=1, source_target_pairs={{0,4},{4,0},{8,12},{12,8},{16,20},{20,16},{24,28},{28,24},{1,5},{5... | collective-permute-start | bytes 3145736 | tf_op jit(solution)/shard_map/s/ppermute | solution.py:89
  12.7 3.2 %collective-permute-done.1 = bf16[256,256]{1,0:T(8,128)(2,1)S(1)} collective-permute-done((bf16[256,256]{1,0:T(8,128)(2,1)S(1)}, bf16[256,256]{1,0:T(8,128)(2,1)S(1)}, u32[]{:S(2)}, u32[]{:S(2)}) %collective-permute-start.1) | collective-permute-done | bytes 131104 | tf_op jit(solution)/shard_map/z0_2/ppermute | solution.py:112
  16.7 1.4 %collective-permute-start.12 = (bf16[256,256]{1,0:T(8,128)(2,1)}, bf16[256,256]{1,0:T(8,128)(2,1)S(1)}, u32[]{:S(2)}, u32[]{:S(2)}) collective-permute-start(bf16[256,256]{1,0:T(8,128)(2,1)} %get-tuple-element.28), channel_id=1, source_target_pairs={{0,4},{4,0},{8,12},{12,8},{16,20},{20,16},{24,28},{28,24},{1,5},{5... | collective-permute-start | bytes 393224 | tf_op jit(solution)/shard_map/c0/ppermute | solution.py:89
  18.4 2.5 %collective-permute-start.4 = (bf16[256,256]{1,0:T(8,128)(2,1)S(1)}, bf16[256,256]{1,0:T(8,128)(2,1)S(1)}, u32[]{:S(2)}, u32[]{:S(2)}) collective-permute-start(bf16[256,256]{1,0:T(8,128)(2,1)S(1)} %get-tuple-element.22), channel_id=1, source_target_pairs={{0,2},{1,3},{2,0},{3,1},{4,6},{5,7},{6,4},{7,5},{8,10},{9,11},{10,... | collective-permute-start | bytes 393224 | tf_op jit(solution)/shard_map/z1_2/ppermute | solution.py:112
  20.8 1.1 %collective-permute-start.5 = (bf16[256,256]{1,0:T(8,128)(2,1)S(1)}, bf16[256,256]{1,0:T(8,128)(2,1)S(1)}, u32[]{:S(2)}, u32[]{:S(2)}) collective-permute-start(bf16[256,256]{1,0:T(8,128)(2,1)S(1)} %get-tuple-element.22), channel_id=1, source_target_pairs={{0,3},{1,2},{2,1},{3,0},{4,7},{5,6},{6,5},{7,4},{8,11},{9,10},{10,... | collective-permute-start | bytes 393224 | tf_op jit(solution)/shard_map/z1_3/ppermute | solution.py:112
  21.9 1.3 %collective-permute-start.13 = (bf16[512,256]{1,0:T(8,128)(2,1)S(1)}, bf16[512,256]{1,0:T(8,128)(2,1)S(1)}, u32[]{:S(2)}, u32[]{:S(2)}) collective-permute-start(bf16[512,256]{1,0:T(8,128)(2,1)S(1)} %pad_maximum_fusion.6), channel_id=1, source_target_pairs={{0,8},{4,12},{8,0},{12,4},{16,24},{20,28},{24,16},{28,20},{1,9},{5... | collective-permute-start | bytes 786440 | tf_op jit(solution)/shard_map/w0_2/ppermute | solution.py:89
  23.2 2.4 %maximum_select_fusion = bf16[512,2048]{1,0:T(8,128)(2,1)S(1)} fusion(bf16[256,2048]{1,0:T(8,128)(2,1)} %collective-permute-done.6, bf16[256,2048]{1,0:T(8,128)(2,1)S(1)} %fusion.2, pred[]{:T(512)S(6)} %eq.16), kind=kLoop, calls=%fused_computation.5 | loop fusion | flops 9437184 | bytes 4194305 | tf_op jit(solution)/shard_map/jit(_where)/select_n | solution.py:82
  26.1 1.3 %collective-permute-start.14 = (bf16[512,256]{1,0:T(8,128)(2,1)S(1)}, bf16[512,256]{1,0:T(8,128)(2,1)S(1)}, u32[]{:S(2)}, u32[]{:S(2)}) collective-permute-start(bf16[512,256]{1,0:T(8,128)(2,1)S(1)} %pad_maximum_fusion.6), channel_id=1, source_target_pairs={{0,16},{4,20},{8,24},{12,28},{16,0},{20,4},{24,8},{28,12},{1,17},{... | collective-permute-start | bytes 786440 | tf_op jit(solution)/shard_map/w0_4/ppermute | solution.py:89
  27.7 2.1 %collective-permute-done.5 = bf16[256,256]{1,0:T(8,128)(2,1)S(1)} collective-permute-done((bf16[256,256]{1,0:T(8,128)(2,1)S(1)}, bf16[256,256]{1,0:T(8,128)(2,1)S(1)}, u32[]{:S(2)}, u32[]{:S(2)}) %collective-permute-start.5) | collective-permute-done | bytes 131104 | tf_op jit(solution)/shard_map/z1_3/ppermute | solution.py:112
  29.9 4.5 %collective-permute-start.7 = (bf16[256,256]{1,0:T(8,128)(2,1)S(1)}, bf16[256,256]{1,0:T(8,128)(2,1)S(1)}, u32[]{:S(2)}, u32[]{:S(2)}) collective-permute-start(bf16[256,256]{1,0:T(8,128)(2,1)S(1)} %get-tuple-element.50), channel_id=1, source_target_pairs={{0,4},{4,0},{8,12},{12,8},{16,20},{20,16},{24,28},{28,24},{1,5},{5... | collective-permute-start | bytes 393224 | tf_op jit(solution)/shard_map/c1/ppermute | solution.py:89
  35.9 1.8 %collective-permute-start.8 = (bf16[512,256]{1,0:T(8,128)(2,1)S(1)}, bf16[512,256]{1,0:T(8,128)(2,1)S(1)}, u32[]{:S(2)}, u32[]{:S(2)}) collective-permute-start(bf16[512,256]{1,0:T(8,128)(2,1)S(1)} %pad_maximum_fusion.5), channel_id=1, source_target_pairs={{0,16},{4,20},{8,24},{12,28},{16,0},{20,4},{24,8},{28,12},{1,17},{... | collective-permute-start | bytes 786440 | tf_op jit(solution)/shard_map/w1_4_0/ppermute | solution.py:89
  38.4 2.0 %collective-permute-start.16 = (bf16[512,256]{1,0:T(8,128)(2,1)S(1)}, bf16[512,256]{1,0:T(8,128)(2,1)S(1)}, u32[]{:S(2)}, u32[]{:S(2)}) collective-permute-start(bf16[512,256]{1,0:T(8,128)(2,1)S(1)} %fusion.8.refs_2_), channel_id=1, source_target_pairs={{0,16},{4,20},{8,24},{12,28},{1,17},{5,21},{9,25},{13,29},{2,18},{... | collective-permute-start | bytes 786440 | tf_op jit(solution)/shard_map/kv0_2/ppermute | solution.py:123
  40.4 3.0 %collective-permute-start.17 = (bf16[512,256]{1,0:T(8,128)(2,1)S(1)}, bf16[512,256]{1,0:T(8,128)(2,1)S(1)}, u32[]{:S(2)}, u32[]{:S(2)}) collective-permute-start(bf16[512,256]{1,0:T(8,128)(2,1)S(1)} %fusion.8.refs_2_), channel_id=1, source_target_pairs={{0,8},{4,12},{8,16},{12,20},{16,24},{20,28},{1,9},{5,13},{9,17},{1... | collective-permute-start | bytes 786440 | tf_op jit(solution)/shard_map/kv0_1/ppermute | solution.py:123
  44.1 9.3 %collective-permute-done.10 = bf16[512,256]{1,0:T(8,128)(2,1)S(1)} collective-permute-done((bf16[512,256]{1,0:T(8,128)(2,1)S(1)}, bf16[512,256]{1,0:T(8,128)(2,1)S(1)}, u32[]{:S(2)}, u32[]{:S(2)}) %collective-permute-start.10) | collective-permute-done | bytes 262176 | tf_op jit(solution)/shard_map/w1_2_1/ppermute | solution.py:89
  54.0 1.4 %collective-permute-start.19 = (bf16[512,256]{1,0:T(8,128)(2,1)S(1)}, bf16[512,256]{1,0:T(8,128)(2,1)S(1)}, u32[]{:S(2)}, u32[]{:S(2)}) collective-permute-start(bf16[512,256]{1,0:T(8,128)(2,1)S(1)} %fusion.7.refs_2_), channel_id=1, source_target_pairs={{0,16},{4,20},{8,24},{12,28},{1,17},{5,21},{9,25},{13,29},{2,18},{... | collective-permute-start | bytes 786440 | tf_op jit(solution)/shard_map/kv1_2/ppermute | solution.py:123
  55.5 4.3 %collective-permute-start.20 = (bf16[512,256]{1,0:T(8,128)(2,1)S(1)}, bf16[512,256]{1,0:T(8,128)(2,1)S(1)}, u32[]{:S(2)}, u32[]{:S(2)}) collective-permute-start(bf16[512,256]{1,0:T(8,128)(2,1)S(1)} %fusion.7.refs_2_), channel_id=1, source_target_pairs={{0,8},{4,12},{8,16},{12,20},{16,24},{20,28},{1,9},{5,13},{9,17},{1... | collective-permute-start | bytes 786440 | tf_op jit(solution)/shard_map/kv1_1/ppermute | solution.py:123
  59.8 5.7 %attend.2 = bf16[2,256,512]{2,1,0:T(8,128)(2,1)S(1)} custom-call(s32[1]{0:T(128)} %bitcast.at_ref, s32[4]{0:T(128)S(1)} %bitcast.40, bf16[256,2048]{1,0:T(8,128)(2,1)S(1)} %bitcast.38, bf16[256,1024]{1,0:T(8,128)(2,1)S(1)} %collective-permute-done.11.other_ref, bf16[512,256]{1,0:T(8,128)(2,1)S(1)} %collective-permute-done.16.refs_0_, ...), custom_call_target="tpu_custom_call" | custom-call | flops 5000000000 | bytes 1048576 | tf_op jit(solution)/shard_map/attend/pallas_call | solution.py:69
  65.5 5.4 %collective-permute-start.18 = (bf16[256,512]{1,0:T(8,128)(2,1)S(1)}, bf16[256,512]{1,0:T(8,128)(2,1)S(1)}, u32[]{:S(2)}, u32[]{:S(2)}) collective-permute-start(bf16[256,512]{1,0:T(8,128)(2,1)S(1)} %get-tuple-element.42), channel_id=1, source_target_pairs={{0,4},{4,0},{8,12},{12,8},{16,20},{20,16},{24,28},{28,24},{1,5},{5... | collective-permute-start | bytes 786440 | tf_op jit(solution)/shard_map/o0/ppermute | solution.py:89
  71.0 5.7 %attend.3 = bf16[2,256,512]{2,1,0:T(8,128)(2,1)S(1)} custom-call(s32[1]{0:T(128)} %bitcast.at_ref, s32[4]{0:T(128)S(1)} %bitcast.41, bf16[256,2048]{1,0:T(8,128)(2,1)S(1)} %bitcast.39, bf16[256,1024]{1,0:T(8,128)(2,1)S(1)} %collective-permute-done.11.other_ref, bf16[512,256]{1,0:T(8,128)(2,1)S(1)} %collective-permute-done.19.refs_0_, ...), custom_call_target="tpu_custom_call" | custom-call | flops 5000000000 | bytes 1048576 | tf_op jit(solution)/shard_map/attend/pallas_call | solution.py:69
  77.0 1.4 %collective-permute-done.21 = bf16[256,512]{1,0:T(8,128)(2,1)S(1)} collective-permute-done((bf16[256,512]{1,0:T(8,128)(2,1)S(1)}, bf16[256,512]{1,0:T(8,128)(2,1)S(1)}, u32[]{:S(2)}, u32[]{:S(2)}) %collective-permute-start.21) | collective-permute-done | bytes 262176 | tf_op jit(solution)/shard_map/o1/ppermute | solution.py:89
  78.5 1.1 %maximum_bitcast_fusion = bf16[1,256,2048]{2,1,0:T(8,128)(2,1)} fusion(bf16[256,1024]{1,0:T(8,128)(2,1)S(1)} %maximum_select_fusion.2, bf16[256,1024]{1,0:T(8,128)(2,1)S(1)} %maximum_select_fusion.1), kind=kLoop, calls=%fused_computation.14 | loop fusion | flops 2097152 | bytes 2097152 | tf_op jit(solution)/shard_map/broadcast_in_dim | solution.py:181
  (64 shorter events, 8.5 us)
Async XLA Ops:
  0.0 15.9 %copy-start.2 = (bf16[1,256,512]{2,1,0:T(8,128)(2,1)S(1)}, bf16[1,256,512]{2,1,0:T(8,128)(2,1)}, u32[]{:S(2)}) copy-start(bf16[1,256,512]{2,1,0:T(8,128)(2,1)} %param.9) | copy-start | bytes 786436
  1.0 11.7 %collective-permute-start = (bf16[256,256]{1,0:T(8,128)(2,1)S(1)}, bf16[256,256]{1,0:T(8,128)(2,1)S(1)}, u32[]{:S(2)}, u32[]{:S(2)}) collective-permute-start(bf16[256,256]{1,0:T(8,128)(2,1)S(1)} %slice.67), channel_id=1, source_target_pairs={{0,3},{1,2},{2,1},{3,0},{4,7},{5,6},{6,5},{7,4},{8,11},{9,10},{10,... | collective-permute-start | bytes 393224 | tf_op jit(solution)/shard_map/z0_3/ppermute | solution.py:112
  5.2 10.7 %collective-permute-start.1 = (bf16[256,256]{1,0:T(8,128)(2,1)S(1)}, bf16[256,256]{1,0:T(8,128)(2,1)S(1)}, u32[]{:S(2)}, u32[]{:S(2)}) collective-permute-start(bf16[256,256]{1,0:T(8,128)(2,1)S(1)} %slice.67), channel_id=1, source_target_pairs={{0,2},{1,3},{2,0},{3,1},{4,6},{5,7},{6,4},{7,5},{8,10},{9,11},{10,... | collective-permute-start | bytes 393224 | tf_op jit(solution)/shard_map/z0_2/ppermute | solution.py:112
  5.2 10.7 %collective-permute-start.2 = (bf16[256,256]{1,0:T(8,128)(2,1)S(1)}, bf16[256,256]{1,0:T(8,128)(2,1)S(1)}, u32[]{:S(2)}, u32[]{:S(2)}) collective-permute-start(bf16[256,256]{1,0:T(8,128)(2,1)S(1)} %slice.67), channel_id=1, source_target_pairs={{0,1},{1,0},{2,3},{3,2},{4,5},{5,4},{6,7},{7,6},{8,9},{9,8},{10,11... | collective-permute-start | bytes 393224 | tf_op jit(solution)/shard_map/z0_1/ppermute | solution.py:112
  9.4 12.5 %collective-permute-start.6 = (bf16[256,2048]{1,0:T(8,128)(2,1)S(1)}, bf16[256,2048]{1,0:T(8,128)(2,1)}, u32[]{:S(2)}, u32[]{:S(2)}) collective-permute-start(bf16[256,2048]{1,0:T(8,128)(2,1)S(1)} %fusion.2), channel_id=1, source_target_pairs={{0,4},{4,0},{8,12},{12,8},{16,20},{20,16},{24,28},{28,24},{1,5},{5... | collective-permute-start | bytes 3145736 | tf_op jit(solution)/shard_map/s/ppermute | solution.py:89
  16.7 4.1 %collective-permute-start.12 = (bf16[256,256]{1,0:T(8,128)(2,1)}, bf16[256,256]{1,0:T(8,128)(2,1)S(1)}, u32[]{:S(2)}, u32[]{:S(2)}) collective-permute-start(bf16[256,256]{1,0:T(8,128)(2,1)} %get-tuple-element.28), channel_id=1, source_target_pairs={{0,4},{4,0},{8,12},{12,8},{16,20},{20,16},{24,28},{28,24},{1,5},{5... | collective-permute-start | bytes 393224 | tf_op jit(solution)/shard_map/c0/ppermute | solution.py:89
  18.2 41.6 %collective-permute-start.11 = (bf16[256,1024]{1,0:T(8,128)(2,1)S(1)}, bf16[256,1024]{1,0:T(8,128)(2,1)S(1)}, u32[]{:S(2)}, u32[]{:S(2)}) collective-permute-start(bf16[256,1024]{1,0:T(8,128)(2,1)S(1)} %pad_maximum_fusion.4), channel_id=1, source_target_pairs={{0,4},{4,0},{8,12},{12,8},{16,20},{20,16},{24,28},{28,24},{1,5},{5... | collective-permute-start | bytes 1572872 | tf_op jit(solution)/shard_map/q/ppermute | solution.py:89
  18.3 7.8 %collective-permute-start.3 = (bf16[256,256]{1,0:T(8,128)(2,1)S(1)}, bf16[256,256]{1,0:T(8,128)(2,1)S(1)}, u32[]{:S(2)}, u32[]{:S(2)}) collective-permute-start(bf16[256,256]{1,0:T(8,128)(2,1)S(1)} %get-tuple-element.22), channel_id=1, source_target_pairs={{0,1},{1,0},{2,3},{3,2},{4,5},{5,4},{6,7},{7,6},{8,9},{9,8},{10,11... | collective-permute-start | bytes 393224 | tf_op jit(solution)/shard_map/z1_1/ppermute | solution.py:112
  18.4 9.0 %collective-permute-start.4 = (bf16[256,256]{1,0:T(8,128)(2,1)S(1)}, bf16[256,256]{1,0:T(8,128)(2,1)S(1)}, u32[]{:S(2)}, u32[]{:S(2)}) collective-permute-start(bf16[256,256]{1,0:T(8,128)(2,1)S(1)} %get-tuple-element.22), channel_id=1, source_target_pairs={{0,2},{1,3},{2,0},{3,1},{4,6},{5,7},{6,4},{7,5},{8,10},{9,11},{10,... | collective-permute-start | bytes 393224 | tf_op jit(solution)/shard_map/z1_2/ppermute | solution.py:112
  20.8 8.9 %collective-permute-start.5 = (bf16[256,256]{1,0:T(8,128)(2,1)S(1)}, bf16[256,256]{1,0:T(8,128)(2,1)S(1)}, u32[]{:S(2)}, u32[]{:S(2)}) collective-permute-start(bf16[256,256]{1,0:T(8,128)(2,1)S(1)} %get-tuple-element.22), channel_id=1, source_target_pairs={{0,3},{1,2},{2,1},{3,0},{4,7},{5,6},{6,5},{7,4},{8,11},{9,10},{10,... | collective-permute-start | bytes 393224 | tf_op jit(solution)/shard_map/z1_3/ppermute | solution.py:112
  21.9 12.5 %collective-permute-start.13 = (bf16[512,256]{1,0:T(8,128)(2,1)S(1)}, bf16[512,256]{1,0:T(8,128)(2,1)S(1)}, u32[]{:S(2)}, u32[]{:S(2)}) collective-permute-start(bf16[512,256]{1,0:T(8,128)(2,1)S(1)} %pad_maximum_fusion.6), channel_id=1, source_target_pairs={{0,8},{4,12},{8,0},{12,4},{16,24},{20,28},{24,16},{28,20},{1,9},{5... | collective-permute-start | bytes 786440 | tf_op jit(solution)/shard_map/w0_2/ppermute | solution.py:89
  26.1 9.2 %collective-permute-start.14 = (bf16[512,256]{1,0:T(8,128)(2,1)S(1)}, bf16[512,256]{1,0:T(8,128)(2,1)S(1)}, u32[]{:S(2)}, u32[]{:S(2)}) collective-permute-start(bf16[512,256]{1,0:T(8,128)(2,1)S(1)} %pad_maximum_fusion.6), channel_id=1, source_target_pairs={{0,16},{4,20},{8,24},{12,28},{16,0},{20,4},{24,8},{28,12},{1,17},{... | collective-permute-start | bytes 786440 | tf_op jit(solution)/shard_map/w0_4/ppermute | solution.py:89
  27.4 8.2 %collective-permute-start.15 = (bf16[512,256]{1,0:T(8,128)(2,1)S(1)}, bf16[512,256]{1,0:T(8,128)(2,1)S(1)}, u32[]{:S(2)}, u32[]{:S(2)}) collective-permute-start(bf16[512,256]{1,0:T(8,128)(2,1)S(1)} %pad_maximum_fusion.6), channel_id=1, source_target_pairs={{0,24},{4,28},{8,16},{12,20},{16,8},{20,12},{24,0},{28,4},{1,25},{... | collective-permute-start | bytes 786440 | tf_op jit(solution)/shard_map/w0_6/ppermute | solution.py:89
  29.9 5.9 %collective-permute-start.7 = (bf16[256,256]{1,0:T(8,128)(2,1)S(1)}, bf16[256,256]{1,0:T(8,128)(2,1)S(1)}, u32[]{:S(2)}, u32[]{:S(2)}) collective-permute-start(bf16[256,256]{1,0:T(8,128)(2,1)S(1)} %get-tuple-element.50), channel_id=1, source_target_pairs={{0,4},{4,0},{8,12},{12,8},{16,20},{20,16},{24,28},{28,24},{1,5},{5... | collective-permute-start | bytes 393224 | tf_op jit(solution)/shard_map/c1/ppermute | solution.py:89
  35.9 7.5 %collective-permute-start.8 = (bf16[512,256]{1,0:T(8,128)(2,1)S(1)}, bf16[512,256]{1,0:T(8,128)(2,1)S(1)}, u32[]{:S(2)}, u32[]{:S(2)}) collective-permute-start(bf16[512,256]{1,0:T(8,128)(2,1)S(1)} %pad_maximum_fusion.5), channel_id=1, source_target_pairs={{0,16},{4,20},{8,24},{12,28},{16,0},{20,4},{24,8},{28,12},{1,17},{... | collective-permute-start | bytes 786440 | tf_op jit(solution)/shard_map/w1_4_0/ppermute | solution.py:89
  37.7 5.7 %collective-permute-start.9 = (bf16[512,256]{1,0:T(8,128)(2,1)S(1)}, bf16[512,256]{1,0:T(8,128)(2,1)S(1)}, u32[]{:S(2)}, u32[]{:S(2)}) collective-permute-start(bf16[512,256]{1,0:T(8,128)(2,1)S(1)} %pad_maximum_fusion.5), channel_id=1, source_target_pairs={{0,8},{4,12},{8,0},{12,4},{16,24},{20,28},{24,16},{28,20},{1,9},{5... | collective-permute-start | bytes 786440 | tf_op jit(solution)/shard_map/w1_2_0/ppermute | solution.py:89
  38.4 21.4 %collective-permute-start.16 = (bf16[512,256]{1,0:T(8,128)(2,1)S(1)}, bf16[512,256]{1,0:T(8,128)(2,1)S(1)}, u32[]{:S(2)}, u32[]{:S(2)}) collective-permute-start(bf16[512,256]{1,0:T(8,128)(2,1)S(1)} %fusion.8.refs_2_), channel_id=1, source_target_pairs={{0,16},{4,20},{8,24},{12,28},{1,17},{5,21},{9,25},{13,29},{2,18},{... | collective-permute-start | bytes 786440 | tf_op jit(solution)/shard_map/kv0_2/ppermute | solution.py:123
  40.4 19.4 %collective-permute-start.17 = (bf16[512,256]{1,0:T(8,128)(2,1)S(1)}, bf16[512,256]{1,0:T(8,128)(2,1)S(1)}, u32[]{:S(2)}, u32[]{:S(2)}) collective-permute-start(bf16[512,256]{1,0:T(8,128)(2,1)S(1)} %fusion.8.refs_2_), channel_id=1, source_target_pairs={{0,8},{4,12},{8,16},{12,20},{16,24},{20,28},{1,9},{5,13},{9,17},{1... | collective-permute-start | bytes 786440 | tf_op jit(solution)/shard_map/kv0_1/ppermute | solution.py:123
  43.4 10.0 %collective-permute-start.10 = (bf16[512,256]{1,0:T(8,128)(2,1)S(1)}, bf16[512,256]{1,0:T(8,128)(2,1)S(1)}, u32[]{:S(2)}, u32[]{:S(2)}) collective-permute-start(bf16[512,256]{1,0:T(8,128)(2,1)S(1)} %collective-permute-done.8), channel_id=1, source_target_pairs={{0,8},{4,12},{8,0},{12,4},{16,24},{20,28},{24,16},{28,20},{1,9},{5... | collective-permute-start | bytes 786440 | tf_op jit(solution)/shard_map/w1_2_1/ppermute | solution.py:89
  44.1 15.7 %copy-start.1 = (s32[1,4]{1,0:T(1,128)S(1)}, s32[1,4]{1,0:T(1,128)}, u32[]{:S(2)}) copy-start(s32[1,4]{1,0:T(1,128)} %param.11) | copy-start | bytes 52
  54.0 16.9 %collective-permute-start.19 = (bf16[512,256]{1,0:T(8,128)(2,1)S(1)}, bf16[512,256]{1,0:T(8,128)(2,1)S(1)}, u32[]{:S(2)}, u32[]{:S(2)}) collective-permute-start(bf16[512,256]{1,0:T(8,128)(2,1)S(1)} %fusion.7.refs_2_), channel_id=1, source_target_pairs={{0,16},{4,20},{8,24},{12,28},{1,17},{5,21},{9,25},{13,29},{2,18},{... | collective-permute-start | bytes 786440 | tf_op jit(solution)/shard_map/kv1_2/ppermute | solution.py:123
  55.5 15.5 %collective-permute-start.20 = (bf16[512,256]{1,0:T(8,128)(2,1)S(1)}, bf16[512,256]{1,0:T(8,128)(2,1)S(1)}, u32[]{:S(2)}, u32[]{:S(2)}) collective-permute-start(bf16[512,256]{1,0:T(8,128)(2,1)S(1)} %fusion.7.refs_2_), channel_id=1, source_target_pairs={{0,8},{4,12},{8,16},{12,20},{16,24},{20,28},{1,9},{5,13},{9,17},{1... | collective-permute-start | bytes 786440 | tf_op jit(solution)/shard_map/kv1_1/ppermute | solution.py:123
  65.5 11.3 %collective-permute-start.18 = (bf16[256,512]{1,0:T(8,128)(2,1)S(1)}, bf16[256,512]{1,0:T(8,128)(2,1)S(1)}, u32[]{:S(2)}, u32[]{:S(2)}) collective-permute-start(bf16[256,512]{1,0:T(8,128)(2,1)S(1)} %get-tuple-element.42), channel_id=1, source_target_pairs={{0,4},{4,0},{8,12},{12,8},{16,20},{20,16},{24,28},{28,24},{1,5},{5... | collective-permute-start | bytes 786440 | tf_op jit(solution)/shard_map/o0/ppermute | solution.py:89
  76.7 1.6 %collective-permute-start.21 = (bf16[256,512]{1,0:T(8,128)(2,1)S(1)}, bf16[256,512]{1,0:T(8,128)(2,1)S(1)}, u32[]{:S(2)}, u32[]{:S(2)}) collective-permute-start(bf16[256,512]{1,0:T(8,128)(2,1)S(1)} %get-tuple-element.44), channel_id=1, source_target_pairs={{0,4},{4,0},{8,12},{12,8},{16,20},{20,16},{24,28},{28,24},{1,5},{5... | collective-permute-start | bytes 786440 | tf_op jit(solution)/shard_map/o1/ppermute | solution.py:89
  (2 other events, 21.0 us)

commit v3 on v2

--- a/solution.py
+++ b/solution.py
@@ -51,6 +51,7 @@
     for b in range(CORES):
         keys = window(b * block, pl.ds(0, HS))
         values = window(b * block, pl.ds(HS, HS))
+        values = jnp.concatenate([values, jnp.ones_like(values)], axis=1)
         for g in range(group):
             own = own_ref[:, pl.ds(pl.multiple_of(((head * CORES + core) * group + g) * HS, HS), HS)]
             column = (head * group + g) * HS
@@ -59,9 +60,8 @@
             score = score + bias_ref[b]
             top = jnp.max(score, axis=-1, keepdims=True)
             weight = jnp.exp2((score - top) * factor)
-            total = jnp.sum(weight, axis=-1, keepdims=True)
             summed = jnp.dot(weight.astype(jnp.bfloat16), values, preferred_element_type=jnp.float32)
-            out_ref[core ^ b, :, g * HS : (g + 1) * HS] = (summed / total).astype(jnp.bfloat16)
+            out_ref[core ^ b, :, g * HS : (g + 1) * HS] = (summed[:, :HS] / summed[:, HS:]).astype(jnp.bfloat16)
 
 
 def attend(head, heads, at, docs, own, other, kvs):
@@ -103,7 +103,7 @@
     chips = n_ctx // CORES
     back = REACH // CORES
 
-    pieces = [slot[:, h * CORES * HS : (h + 1) * CORES * HS] for h in range(heads)]
+    pieces = [slot[:, : CORES * HS]]
 
     def over_dp(h, piece):
         slots = [piece]
@@ -129,18 +129,11 @@
         * lax.rsqrt(jnp.mean(xf * xf, axis=-1, keepdims=True) + 1e-05)
         * norm_gain.astype(jnp.float32)
     ).astype(jnp.bfloat16)
-    scaled = both_cores(core, scaled, exchange(scaled, 1, n_ctx, "s"), 0)
-    columns = [
-        jnp.concatenate(
-            [lax.dynamic_slice_in_dim(scaled, (at ^ (o * CORES) ^ c) * rows, rows, 1) for c in range(CORES)], axis=1
-        )
-        for o in range(chips)
-    ]
+    slots, scaled = lax.optimization_barrier((slots, scaled))
+    slot = after(slot, scaled)
+    pieces += [slot[:, h * CORES * HS : (h + 1) * CORES * HS] for h in range(1, heads)]
+    scaled_other = exchange(scaled, 1, n_ctx, "s")
     share = queries.shape[2] // (heads * CORES)
-    q_other = jnp.concatenate(
-        [lax.dynamic_slice_in_dim(queries[0], (h * CORES + 1 - core) * share, share, 1) for h in range(heads)], axis=1
-    )
-    q_other = exchange(q_other, 1, n_ctx, "q")
 
     bits = [CORES << i for i in reversed(range(chips.bit_length() - 1))]
     window = []
@@ -152,12 +145,28 @@
         if h + 1 < heads:
             piece, theirs = lax.optimization_barrier((pieces[h + 1], theirs))
             slots = over_dp(h + 1, piece)
+        if h:
+            q_all = after(queries[0], theirs)
+            q_other = jnp.concatenate(
+                [lax.dynamic_slice_in_dim(q_all, (i * CORES + 1 - core) * share, share, 1) for i in range(heads)], axis=1
+            )
+            q_other = exchange(q_other, 1, n_ctx, "q")
         parts, order = [jnp.concatenate([mine, exchange(theirs, 1, n_ctx, f"c{h}")], axis=0)], [0]
         if h == 0:
+            parts[0], scaled_other = lax.optimization_barrier((parts[0], scaled_other))
+            both = both_cores(core, scaled, scaled_other, 0)
+            columns = [
+                jnp.concatenate(
+                    [lax.dynamic_slice_in_dim(both, (at ^ (o * CORES) ^ c) * rows, rows, 1) for c in range(CORES)],
+                    axis=1,
+                )
+                for o in range(chips)
+            ]
             for o in range(CORES, n_ctx, CORES):
                 parts.append(exchange(parts[0], o, n_ctx, f"w{h}_{o}"))
                 order.append(o)
             slots, columns = lax.optimization_barrier((slots, columns))
+            parts = list(lax.optimization_barrier(parts))
         else:
             for bit in bits:
                 for i, (o, p) in enumerate(zip(list(order), list(parts))):

time: 80 us -> 78.3 us (0.979); the launches traced: 79.5 us -> 76.8 us
  waiting for transfers between devices: 16.5 us -> 20.1 us
  starting transfers between devices: 36.8 us -> 34.2 us
  other arithmetic: 8.65 us -> 6.49 us
  Pallas kernels: 11.4 us -> 9.82 us
    ppermute x6, waiting for transfers between devices: 5.26 us -> 9.29 us  [over_dp(): slots.append(lax.ppermute(piece, 'dp', [(i, i ^ k) for i in range(n_dp)]))]
    ppermute x12, starting transfers between devices: 17.9 us -> 15.2 us  [exchange(): return lax.ppermute(x, 'ctx', [(i, i ^ bit) for i in range(size)])]
    pallas_call x2, Pallas kernels: 11.4 us -> 9.82 us  [attend(): pl.pallas_call(functools.partial(attend_kernel, head), out_shape=jax.Shap...]
    select_n x3, other arithmetic: 2.66 us -> 1.24 us  [both_cores(): jnp.where(core == 0, jnp.concatenate([own, other], axis), jnp.concatenate...]
    slice x0 -> x1, local copies, waits for them, and re-layouts: none -> 0.98 us  [local(): pieces = [slot[:, :CORES * HS]]]
    slice x1, local copies, waits for them, and re-layouts: 0.98 us -> 0.01 us  [local(): slot[:, h * CORES * HS:(h + 1) * CORES * HS]]
  transfers between devices with their start and end apart: 22 -> 22, of which waited for: 5 -> 6; matrix products, arithmetic and copies ran while one was open for 14% -> 11% of each run, Pallas kernels for 14% -> 13%
where the time goes in v3:
time: 78.3 us; the launch traced here: 76.8 us
  starting transfers between devices  34.2 us (44%)
  waiting for transfers between devices  20.1 us (26%)
  Pallas kernels  9.82 us (13%)
  other arithmetic  6.49 us (8%)
  matrix products  2.4 us (3%)
  local copies, waits for them, and re-layouts  2.13 us (3%)
  between operations  1.7 us (2%)
    ppermute x12, starting transfers between devices, exchange(): return lax.ppermute(x, 'ctx', [(i, i ^ bit) for i in range(size)])  15.2 us
    ppermute x12, waiting for transfers between devices, exchange(): return lax.ppermute(x, 'ctx', [(i, i ^ bit) for i in range(size)])  10.8 us
    ppermute x4, starting transfers between devices, forward(): lax.ppermute(x, 'ctx', [(i, i + by * CORES) for i in range(n_ctx - by * C...  10.6 us
    pallas_call x2, Pallas kernels, attend(): pl.pallas_call(functools.partial(attend_kernel, head), out_shape=jax.Shap...  9.82 us
    ppermute x6, waiting for transfers between devices, over_dp(): slots.append(lax.ppermute(piece, 'dp', [(i, i ^ k) for i in range(n_dp)]))  9.29 us
    ppermute x6, starting transfers between devices, over_dp(): slots.append(lax.ppermute(piece, 'dp', [(i, i ^ k) for i in range(n_dp)]))  8.44 us
    dot_general x8, matrix products, local(): jnp.dot(columns[o // CORES], part, preferred_element_type=jnp.float32)  2.4 us
  transfers between devices with their start and end apart: 22, of which 6 were waited for; matrix products, arithmetic and copies ran while one was open for 11% of the time, Pallas kernels for 13%

profile of v3, /device:TPU:1, one launch (start us, length us, event | category | flops | bytes accessed | tf_op | source)
XLA Modules:
  0.0 76.8 jit_solution(8469037086141896240)
XLA Ops:
  1.0 2.2 %collective-permute-start = (bf16[256,256]{1,0:T(8,128)(2,1)S(1)}, bf16[256,256]{1,0:T(8,128)(2,1)S(1)}, u32[]{:S(2)}, u32[]{:S(2)}) collective-permute-start(bf16[256,256]{1,0:T(8,128)(2,1)S(1)} %slice.66), channel_id=1, source_target_pairs={{0,1},{1,0},{2,3},{3,2},{4,5},{5,4},{6,7},{7,6},{8,9},{9,8},{10,11... | collective-permute-start | bytes 393224 | tf_op jit(solution)/shard_map/z0_1/ppermute | solution.py:112
  3.2 2.3 %collective-permute-start.1 = (bf16[256,256]{1,0:T(8,128)(2,1)S(1)}, bf16[256,256]{1,0:T(8,128)(2,1)S(1)}, u32[]{:S(2)}, u32[]{:S(2)}) collective-permute-start(bf16[256,256]{1,0:T(8,128)(2,1)S(1)} %slice.66), channel_id=1, source_target_pairs={{0,2},{1,3},{2,0},{3,1},{4,6},{5,7},{6,4},{7,5},{8,10},{9,11},{10,... | collective-permute-start | bytes 393224 | tf_op jit(solution)/shard_map/z0_2/ppermute | solution.py:112
  6.2 1.5 %fusion = f32[256]{0:T(256)S(1)} fusion(bf16[1,256,2048]{2,1,0:T(8,128)(2,1)} %param.6), kind=kLoop, calls=%fused_computation.2 | loop fusion | flops 1572608 | bytes 1049600 | tf_op jit(solution)/shard_map/reduce_sum | solution.py:129
  7.7 1.5 %fusion.2 = bf16[256,2048]{1,0:T(8,128)(2,1)S(1)} fusion(bf16[1,256,2048]{2,1,0:T(8,128)(2,1)} %param.6, f32[2048]{0:T(1024)S(1)} %convert_element_type.20, f32[256]{0:T(256)S(1)} %add_rsqrt_fusion), kind=kLoop, calls=%fused_computation.4 | loop fusion | flops 2097152 | bytes 2106368 | tf_op jit(solution)/shard_map/convert_element_type | solution.py:131
  9.3 4.7 %collective-permute-done.2 = bf16[256,256]{1,0:T(8,128)(2,1)S(1)} collective-permute-done((bf16[256,256]{1,0:T(8,128)(2,1)S(1)}, bf16[256,256]{1,0:T(8,128)(2,1)S(1)}, u32[]{:S(2)}, u32[]{:S(2)}) %collective-permute-start.2) | collective-permute-done | bytes 131104 | tf_op jit(solution)/shard_map/z0_3/ppermute | solution.py:112
  13.9 3.1 %collective-permute-start.7 = (bf16[256,2048]{1,0:T(8,128)(2,1)S(1)}, bf16[256,2048]{1,0:T(8,128)(2,1)S(1)}, u32[]{:S(2)}, u32[]{:S(2)}) collective-permute-start(bf16[256,2048]{1,0:T(8,128)(2,1)S(1)} %fusion.2), channel_id=1, source_target_pairs={{0,4},{4,0},{8,12},{12,8},{16,20},{20,16},{24,28},{28,24},{1,5},{5... | collective-permute-start | bytes 3145736 | tf_op jit(solution)/shard_map/s/ppermute | solution.py:89
  19.3 1.7 %collective-permute-start.3 = (bf16[256,256]{1,0:T(8,128)(2,1)S(1)}, bf16[256,256]{1,0:T(8,128)(2,1)S(1)}, u32[]{:S(2)}, u32[]{:S(2)}) collective-permute-start(bf16[256,256]{1,0:T(8,128)(2,1)S(1)} %slice.51), channel_id=1, source_target_pairs={{0,1},{1,0},{2,3},{3,2},{4,5},{5,4},{6,7},{7,6},{8,9},{9,8},{10,11... | collective-permute-start | bytes 393224 | tf_op jit(solution)/shard_map/z1_1/ppermute | solution.py:112
  21.1 1.1 %collective-permute-start.4 = (bf16[256,256]{1,0:T(8,128)(2,1)S(1)}, bf16[256,256]{1,0:T(8,128)(2,1)S(1)}, u32[]{:S(2)}, u32[]{:S(2)}) collective-permute-start(bf16[256,256]{1,0:T(8,128)(2,1)S(1)} %slice.51), channel_id=1, source_target_pairs={{0,2},{1,3},{2,0},{3,1},{4,6},{5,7},{6,4},{7,5},{8,10},{9,11},{10,... | collective-permute-start | bytes 393224 | tf_op jit(solution)/shard_map/z1_2/ppermute | solution.py:112
  22.1 1.1 %collective-permute-start.5 = (bf16[256,256]{1,0:T(8,128)(2,1)S(1)}, bf16[256,256]{1,0:T(8,128)(2,1)S(1)}, u32[]{:S(2)}, u32[]{:S(2)}) collective-permute-start(bf16[256,256]{1,0:T(8,128)(2,1)S(1)} %slice.51), channel_id=1, source_target_pairs={{0,3},{1,2},{2,1},{3,0},{4,7},{5,6},{6,5},{7,4},{8,11},{9,10},{10,... | collective-permute-start | bytes 393224 | tf_op jit(solution)/shard_map/z1_3/ppermute | solution.py:112
  23.3 1.3 %collective-permute-start.13 = (bf16[512,256]{1,0:T(8,128)(2,1)S(1)}, bf16[512,256]{1,0:T(8,128)(2,1)S(1)}, u32[]{:S(2)}, u32[]{:S(2)}) collective-permute-start(bf16[512,256]{1,0:T(8,128)(2,1)S(1)} %pad_maximum_fusion.5), channel_id=1, source_target_pairs={{0,8},{4,12},{8,0},{12,4},{16,24},{20,28},{24,16},{28,20},{1,9},{5... | collective-permute-start | bytes 786440 | tf_op jit(solution)/shard_map/w0_2/ppermute | solution.py:89
  24.6 1.2 %collective-permute-start.14 = (bf16[512,256]{1,0:T(8,128)(2,1)S(1)}, bf16[512,256]{1,0:T(8,128)(2,1)S(1)}, u32[]{:S(2)}, u32[]{:S(2)}) collective-permute-start(bf16[512,256]{1,0:T(8,128)(2,1)S(1)} %pad_maximum_fusion.5), channel_id=1, source_target_pairs={{0,16},{4,20},{8,24},{12,28},{16,0},{20,4},{24,8},{28,12},{1,17},{... | collective-permute-start | bytes 786440 | tf_op jit(solution)/shard_map/w0_4/ppermute | solution.py:89
  27.5 4.6 %collective-permute-done.5 = bf16[256,256]{1,0:T(8,128)(2,1)S(1)} collective-permute-done((bf16[256,256]{1,0:T(8,128)(2,1)S(1)}, bf16[256,256]{1,0:T(8,128)(2,1)S(1)}, u32[]{:S(2)}, u32[]{:S(2)}) %collective-permute-start.5) | collective-permute-done | bytes 131104 | tf_op jit(solution)/shard_map/z1_3/ppermute | solution.py:112
  32.3 2.5 %collective-permute-start.8 = (bf16[256,256]{1,0:T(8,128)(2,1)S(1)}, bf16[256,256]{1,0:T(8,128)(2,1)S(1)}, u32[]{:S(2)}, u32[]{:S(2)}) collective-permute-start(bf16[256,256]{1,0:T(8,128)(2,1)S(1)} %get-tuple-element.74), channel_id=1, source_target_pairs={{0,4},{4,0},{8,12},{12,8},{16,20},{20,16},{24,28},{28,24},{1,5},{5... | collective-permute-start | bytes 393224 | tf_op jit(solution)/shard_map/c1/ppermute | solution.py:89
  35.9 1.3 %collective-permute-start.9 = (bf16[512,256]{1,0:T(8,128)(2,1)S(1)}, bf16[512,256]{1,0:T(8,128)(2,1)S(1)}, u32[]{:S(2)}, u32[]{:S(2)}) collective-permute-start(bf16[512,256]{1,0:T(8,128)(2,1)S(1)} %pad_maximum_fusion.6), channel_id=1, source_target_pairs={{0,16},{4,20},{8,24},{12,28},{16,0},{20,4},{24,8},{28,12},{1,17},{... | collective-permute-start | bytes 786440 | tf_op jit(solution)/shard_map/w1_4_0/ppermute | solution.py:89
  37.2 1.2 %collective-permute-start.10 = (bf16[512,256]{1,0:T(8,128)(2,1)S(1)}, bf16[512,256]{1,0:T(8,128)(2,1)S(1)}, u32[]{:S(2)}, u32[]{:S(2)}) collective-permute-start(bf16[512,256]{1,0:T(8,128)(2,1)S(1)} %pad_maximum_fusion.6), channel_id=1, source_target_pairs={{0,8},{4,12},{8,0},{12,4},{16,24},{20,28},{24,16},{28,20},{1,9},{5... | collective-permute-start | bytes 786440 | tf_op jit(solution)/shard_map/w1_2_0/ppermute | solution.py:89
  39.6 2.1 %collective-permute-start.16 = (bf16[512,256]{1,0:T(8,128)(2,1)S(1)}, bf16[512,256]{1,0:T(8,128)(2,1)S(1)}, u32[]{:S(2)}, u32[]{:S(2)}) collective-permute-start(bf16[512,256]{1,0:T(8,128)(2,1)S(1)} %fusion.8.refs_2_), channel_id=1, source_target_pairs={{0,16},{4,20},{8,24},{12,28},{1,17},{5,21},{9,25},{13,29},{2,18},{... | collective-permute-start | bytes 786440 | tf_op jit(solution)/shard_map/kv0_2/ppermute | solution.py:123
  41.8 2.2 %collective-permute-start.17 = (bf16[512,256]{1,0:T(8,128)(2,1)S(1)}, bf16[512,256]{1,0:T(8,128)(2,1)S(1)}, u32[]{:S(2)}, u32[]{:S(2)}) collective-permute-start(bf16[512,256]{1,0:T(8,128)(2,1)S(1)} %fusion.8.refs_2_), channel_id=1, source_target_pairs={{0,8},{4,12},{8,16},{12,20},{16,24},{20,28},{1,9},{5,13},{9,17},{1... | collective-permute-start | bytes 786440 | tf_op jit(solution)/shard_map/kv0_1/ppermute | solution.py:123
  44.4 1.2 %collective-permute-start.11 = (bf16[512,256]{1,0:T(8,128)(2,1)S(1)}, bf16[512,256]{1,0:T(8,128)(2,1)S(1)}, u32[]{:S(2)}, u32[]{:S(2)}) collective-permute-start(bf16[512,256]{1,0:T(8,128)(2,1)S(1)} %collective-permute-done.9), channel_id=1, source_target_pairs={{0,8},{4,12},{8,0},{12,4},{16,24},{20,28},{24,16},{28,20},{1,9},{5... | collective-permute-start | bytes 786440 | tf_op jit(solution)/shard_map/w1_2_1/ppermute | solution.py:89
  46.2 8.6 %collective-permute-done.11 = bf16[512,256]{1,0:T(8,128)(2,1)S(1)} collective-permute-done((bf16[512,256]{1,0:T(8,128)(2,1)S(1)}, bf16[512,256]{1,0:T(8,128)(2,1)S(1)}, u32[]{:S(2)}, u32[]{:S(2)}) %collective-permute-start.11) | collective-permute-done | bytes 262176 | tf_op jit(solution)/shard_map/w1_2_1/ppermute | solution.py:89
  55.4 2.0 %collective-permute-start.19 = (bf16[512,256]{1,0:T(8,128)(2,1)S(1)}, bf16[512,256]{1,0:T(8,128)(2,1)S(1)}, u32[]{:S(2)}, u32[]{:S(2)}) collective-permute-start(bf16[512,256]{1,0:T(8,128)(2,1)S(1)} %fusion.7.refs_2_), channel_id=1, source_target_pairs={{0,16},{4,20},{8,24},{12,28},{1,17},{5,21},{9,25},{13,29},{2,18},{... | collective-permute-start | bytes 786440 | tf_op jit(solution)/shard_map/kv1_2/ppermute | solution.py:123
  57.4 4.3 %collective-permute-start.20 = (bf16[512,256]{1,0:T(8,128)(2,1)S(1)}, bf16[512,256]{1,0:T(8,128)(2,1)S(1)}, u32[]{:S(2)}, u32[]{:S(2)}) collective-permute-start(bf16[512,256]{1,0:T(8,128)(2,1)S(1)} %fusion.7.refs_2_), channel_id=1, source_target_pairs={{0,8},{4,12},{8,16},{12,20},{16,24},{20,28},{1,9},{5,13},{9,17},{1... | collective-permute-start | bytes 786440 | tf_op jit(solution)/shard_map/kv1_1/ppermute | solution.py:123
  61.7 4.9 %attend.2 = bf16[2,256,512]{2,1,0:T(8,128)(2,1)S(1)} custom-call(s32[1]{0:T(128)} %bitcast.at_ref, s32[4]{0:T(128)S(1)} %bitcast.38, bf16[256,2048]{1,0:T(8,128)(2,1)S(1)} %bitcast.36, bf16[256,1024]{1,0:T(8,128)(2,1)S(1)} %collective-permute-done.12.other_ref, bf16[512,256]{1,0:T(8,128)(2,1)S(1)} %collective-permute-done.16.refs_0_, ...), custom_call_target="tpu_custom_call" | custom-call | flops 5000000000 | bytes 1048576 | tf_op jit(solution)/shard_map/attend/pallas_call | solution.py:69
  66.7 2.2 %collective-permute-start.18 = (bf16[256,512]{1,0:T(8,128)(2,1)S(1)}, bf16[256,512]{1,0:T(8,128)(2,1)S(1)}, u32[]{:S(2)}, u32[]{:S(2)}) collective-permute-start(bf16[256,512]{1,0:T(8,128)(2,1)S(1)} %get-tuple-element.66), channel_id=1, source_target_pairs={{0,4},{4,0},{8,12},{12,8},{16,20},{20,16},{24,28},{28,24},{1,5},{5... | collective-permute-start | bytes 786440 | tf_op jit(solution)/shard_map/o0/ppermute | solution.py:89
  68.9 4.9 %attend.3 = bf16[2,256,512]{2,1,0:T(8,128)(2,1)S(1)} custom-call(s32[1]{0:T(128)} %bitcast.at_ref, s32[4]{0:T(128)S(1)} %bitcast.39, bf16[256,2048]{1,0:T(8,128)(2,1)S(1)} %bitcast.37, bf16[256,1024]{1,0:T(8,128)(2,1)S(1)} %collective-permute-done.12.other_ref, bf16[512,256]{1,0:T(8,128)(2,1)S(1)} %collective-permute-done.19.refs_0_, ...), custom_call_target="tpu_custom_call" | custom-call | flops 5000000000 | bytes 1048576 | tf_op jit(solution)/shard_map/attend/pallas_call | solution.py:69
  (67 shorter events, 11.3 us)
Async XLA Ops:
  0.0 19.0 %copy-start.2 = (bf16[1,256,512]{2,1,0:T(8,128)(2,1)S(1)}, bf16[1,256,512]{2,1,0:T(8,128)(2,1)}, u32[]{:S(2)}) copy-start(bf16[1,256,512]{2,1,0:T(8,128)(2,1)} %param.9) | copy-start | bytes 786436
  0.0 17.1 %copy-start.3 = (s32[2]{0:T(128)S(1)}, s32[2]{0:T(128)}, u32[]{:S(2)}) copy-start(s32[2]{0:T(128)} %param.10) | copy-start | bytes 28
  1.0 8.3 %collective-permute-start = (bf16[256,256]{1,0:T(8,128)(2,1)S(1)}, bf16[256,256]{1,0:T(8,128)(2,1)S(1)}, u32[]{:S(2)}, u32[]{:S(2)}) collective-permute-start(bf16[256,256]{1,0:T(8,128)(2,1)S(1)} %slice.66), channel_id=1, source_target_pairs={{0,1},{1,0},{2,3},{3,2},{4,5},{5,4},{6,7},{7,6},{8,9},{9,8},{10,11... | collective-permute-start | bytes 393224 | tf_op jit(solution)/shard_map/z0_1/ppermute | solution.py:112
  3.2 6.1 %collective-permute-start.1 = (bf16[256,256]{1,0:T(8,128)(2,1)S(1)}, bf16[256,256]{1,0:T(8,128)(2,1)S(1)}, u32[]{:S(2)}, u32[]{:S(2)}) collective-permute-start(bf16[256,256]{1,0:T(8,128)(2,1)S(1)} %slice.66), channel_id=1, source_target_pairs={{0,2},{1,3},{2,0},{3,1},{4,6},{5,7},{6,4},{7,5},{8,10},{9,11},{10,... | collective-permute-start | bytes 393224 | tf_op jit(solution)/shard_map/z0_2/ppermute | solution.py:112
  5.5 8.4 %collective-permute-start.2 = (bf16[256,256]{1,0:T(8,128)(2,1)S(1)}, bf16[256,256]{1,0:T(8,128)(2,1)S(1)}, u32[]{:S(2)}, u32[]{:S(2)}) collective-permute-start(bf16[256,256]{1,0:T(8,128)(2,1)S(1)} %slice.66), channel_id=1, source_target_pairs={{0,3},{1,2},{2,1},{3,0},{4,7},{5,6},{6,5},{7,4},{8,11},{9,10},{10,... | collective-permute-start | bytes 393224 | tf_op jit(solution)/shard_map/z0_3/ppermute | solution.py:112
  13.9 9.3 %collective-permute-start.7 = (bf16[256,2048]{1,0:T(8,128)(2,1)S(1)}, bf16[256,2048]{1,0:T(8,128)(2,1)S(1)}, u32[]{:S(2)}, u32[]{:S(2)}) collective-permute-start(bf16[256,2048]{1,0:T(8,128)(2,1)S(1)} %fusion.2), channel_id=1, source_target_pairs={{0,4},{4,0},{8,12},{12,8},{16,20},{20,16},{24,28},{28,24},{1,5},{5... | collective-permute-start | bytes 3145736 | tf_op jit(solution)/shard_map/s/ppermute | solution.py:89
  19.2 4.1 %collective-permute-start.6 = (bf16[256,256]{1,0:T(8,128)(2,1)S(1)}, bf16[256,256]{1,0:T(8,128)(2,1)S(1)}, u32[]{:S(2)}, u32[]{:S(2)}) collective-permute-start(bf16[256,256]{1,0:T(8,128)(2,1)S(1)} %get-tuple-element.37), channel_id=1, source_target_pairs={{0,4},{4,0},{8,12},{12,8},{16,20},{20,16},{24,28},{28,24},{1,5},{5... | collective-permute-start | bytes 393224 | tf_op jit(solution)/shard_map/c0/ppermute | solution.py:89
  19.3 8.0 %collective-permute-start.3 = (bf16[256,256]{1,0:T(8,128)(2,1)S(1)}, bf16[256,256]{1,0:T(8,128)(2,1)S(1)}, u32[]{:S(2)}, u32[]{:S(2)}) collective-permute-start(bf16[256,256]{1,0:T(8,128)(2,1)S(1)} %slice.51), channel_id=1, source_target_pairs={{0,1},{1,0},{2,3},{3,2},{4,5},{5,4},{6,7},{7,6},{8,9},{9,8},{10,11... | collective-permute-start | bytes 393224 | tf_op jit(solution)/shard_map/z1_1/ppermute | solution.py:112
  21.1 6.5 %collective-permute-start.4 = (bf16[256,256]{1,0:T(8,128)(2,1)S(1)}, bf16[256,256]{1,0:T(8,128)(2,1)S(1)}, u32[]{:S(2)}, u32[]{:S(2)}) collective-permute-start(bf16[256,256]{1,0:T(8,128)(2,1)S(1)} %slice.51), channel_id=1, source_target_pairs={{0,2},{1,3},{2,0},{3,1},{4,6},{5,7},{6,4},{7,5},{8,10},{9,11},{10,... | collective-permute-start | bytes 393224 | tf_op jit(solution)/shard_map/z1_2/ppermute | solution.py:112
  22.1 10.0 %collective-permute-start.5 = (bf16[256,256]{1,0:T(8,128)(2,1)S(1)}, bf16[256,256]{1,0:T(8,128)(2,1)S(1)}, u32[]{:S(2)}, u32[]{:S(2)}) collective-permute-start(bf16[256,256]{1,0:T(8,128)(2,1)S(1)} %slice.51), channel_id=1, source_target_pairs={{0,3},{1,2},{2,1},{3,0},{4,7},{5,6},{6,5},{7,4},{8,11},{9,10},{10,... | collective-permute-start | bytes 393224 | tf_op jit(solution)/shard_map/z1_3/ppermute | solution.py:112
  23.3 13.9 %collective-permute-start.13 = (bf16[512,256]{1,0:T(8,128)(2,1)S(1)}, bf16[512,256]{1,0:T(8,128)(2,1)S(1)}, u32[]{:S(2)}, u32[]{:S(2)}) collective-permute-start(bf16[512,256]{1,0:T(8,128)(2,1)S(1)} %pad_maximum_fusion.5), channel_id=1, source_target_pairs={{0,8},{4,12},{8,0},{12,4},{16,24},{20,28},{24,16},{28,20},{1,9},{5... | collective-permute-start | bytes 786440 | tf_op jit(solution)/shard_map/w0_2/ppermute | solution.py:89
  24.6 13.8 %collective-permute-start.14 = (bf16[512,256]{1,0:T(8,128)(2,1)S(1)}, bf16[512,256]{1,0:T(8,128)(2,1)S(1)}, u32[]{:S(2)}, u32[]{:S(2)}) collective-permute-start(bf16[512,256]{1,0:T(8,128)(2,1)S(1)} %pad_maximum_fusion.5), channel_id=1, source_target_pairs={{0,16},{4,20},{8,24},{12,28},{16,0},{20,4},{24,8},{28,12},{1,17},{... | collective-permute-start | bytes 786440 | tf_op jit(solution)/shard_map/w0_4/ppermute | solution.py:89
  27.3 11.1 %collective-permute-start.15 = (bf16[512,256]{1,0:T(8,128)(2,1)S(1)}, bf16[512,256]{1,0:T(8,128)(2,1)S(1)}, u32[]{:S(2)}, u32[]{:S(2)}) collective-permute-start(bf16[512,256]{1,0:T(8,128)(2,1)S(1)} %pad_maximum_fusion.5), channel_id=1, source_target_pairs={{0,24},{4,28},{8,16},{12,20},{16,8},{20,12},{24,0},{28,4},{1,25},{... | collective-permute-start | bytes 786440 | tf_op jit(solution)/shard_map/w0_6/ppermute | solution.py:89
  32.3 3.5 %collective-permute-start.8 = (bf16[256,256]{1,0:T(8,128)(2,1)S(1)}, bf16[256,256]{1,0:T(8,128)(2,1)S(1)}, u32[]{:S(2)}, u32[]{:S(2)}) collective-permute-start(bf16[256,256]{1,0:T(8,128)(2,1)S(1)} %get-tuple-element.74), channel_id=1, source_target_pairs={{0,4},{4,0},{8,12},{12,8},{16,20},{20,16},{24,28},{28,24},{1,5},{5... | collective-permute-start | bytes 393224 | tf_op jit(solution)/shard_map/c1/ppermute | solution.py:89
  35.0 26.7 %collective-permute-start.12 = (bf16[256,1024]{1,0:T(8,128)(2,1)S(1)}, bf16[256,1024]{1,0:T(8,128)(2,1)S(1)}, u32[]{:S(2)}, u32[]{:S(2)}) collective-permute-start(bf16[256,1024]{1,0:T(8,128)(2,1)S(1)} %pad_maximum_fusion.4), channel_id=1, source_target_pairs={{0,4},{4,0},{8,12},{12,8},{16,20},{20,16},{24,28},{28,24},{1,5},{5... | collective-permute-start | bytes 1572872 | tf_op jit(solution)/shard_map/q/ppermute | solution.py:89
  35.9 8.1 %collective-permute-start.9 = (bf16[512,256]{1,0:T(8,128)(2,1)S(1)}, bf16[512,256]{1,0:T(8,128)(2,1)S(1)}, u32[]{:S(2)}, u32[]{:S(2)}) collective-permute-start(bf16[512,256]{1,0:T(8,128)(2,1)S(1)} %pad_maximum_fusion.6), channel_id=1, source_target_pairs={{0,16},{4,20},{8,24},{12,28},{16,0},{20,4},{24,8},{28,12},{1,17},{... | collective-permute-start | bytes 786440 | tf_op jit(solution)/shard_map/w1_4_0/ppermute | solution.py:89
  37.2 7.2 %collective-permute-start.10 = (bf16[512,256]{1,0:T(8,128)(2,1)S(1)}, bf16[512,256]{1,0:T(8,128)(2,1)S(1)}, u32[]{:S(2)}, u32[]{:S(2)}) collective-permute-start(bf16[512,256]{1,0:T(8,128)(2,1)S(1)} %pad_maximum_fusion.6), channel_id=1, source_target_pairs={{0,8},{4,12},{8,0},{12,4},{16,24},{20,28},{24,16},{28,20},{1,9},{5... | collective-permute-start | bytes 786440 | tf_op jit(solution)/shard_map/w1_2_0/ppermute | solution.py:89
  39.6 22.1 %collective-permute-start.16 = (bf16[512,256]{1,0:T(8,128)(2,1)S(1)}, bf16[512,256]{1,0:T(8,128)(2,1)S(1)}, u32[]{:S(2)}, u32[]{:S(2)}) collective-permute-start(bf16[512,256]{1,0:T(8,128)(2,1)S(1)} %fusion.8.refs_2_), channel_id=1, source_target_pairs={{0,16},{4,20},{8,24},{12,28},{1,17},{5,21},{9,25},{13,29},{2,18},{... | collective-permute-start | bytes 786440 | tf_op jit(solution)/shard_map/kv0_2/ppermute | solution.py:123
  41.8 19.9 %collective-permute-start.17 = (bf16[512,256]{1,0:T(8,128)(2,1)S(1)}, bf16[512,256]{1,0:T(8,128)(2,1)S(1)}, u32[]{:S(2)}, u32[]{:S(2)}) collective-permute-start(bf16[512,256]{1,0:T(8,128)(2,1)S(1)} %fusion.8.refs_2_), channel_id=1, source_target_pairs={{0,8},{4,12},{8,16},{12,20},{16,24},{20,28},{1,9},{5,13},{9,17},{1... | collective-permute-start | bytes 786440 | tf_op jit(solution)/shard_map/kv0_1/ppermute | solution.py:123
  44.4 10.4 %collective-permute-start.11 = (bf16[512,256]{1,0:T(8,128)(2,1)S(1)}, bf16[512,256]{1,0:T(8,128)(2,1)S(1)}, u32[]{:S(2)}, u32[]{:S(2)}) collective-permute-start(bf16[512,256]{1,0:T(8,128)(2,1)S(1)} %collective-permute-done.9), channel_id=1, source_target_pairs={{0,8},{4,12},{8,0},{12,4},{16,24},{20,28},{24,16},{28,20},{1,9},{5... | collective-permute-start | bytes 786440 | tf_op jit(solution)/shard_map/w1_2_1/ppermute | solution.py:89
  55.4 13.5 %collective-permute-start.19 = (bf16[512,256]{1,0:T(8,128)(2,1)S(1)}, bf16[512,256]{1,0:T(8,128)(2,1)S(1)}, u32[]{:S(2)}, u32[]{:S(2)}) collective-permute-start(bf16[512,256]{1,0:T(8,128)(2,1)S(1)} %fusion.7.refs_2_), channel_id=1, source_target_pairs={{0,16},{4,20},{8,24},{12,28},{1,17},{5,21},{9,25},{13,29},{2,18},{... | collective-permute-start | bytes 786440 | tf_op jit(solution)/shard_map/kv1_2/ppermute | solution.py:123
  57.4 11.5 %collective-permute-start.20 = (bf16[512,256]{1,0:T(8,128)(2,1)S(1)}, bf16[512,256]{1,0:T(8,128)(2,1)S(1)}, u32[]{:S(2)}, u32[]{:S(2)}) collective-permute-start(bf16[512,256]{1,0:T(8,128)(2,1)S(1)} %fusion.7.refs_2_), channel_id=1, source_target_pairs={{0,8},{4,12},{8,16},{12,20},{16,24},{20,28},{1,9},{5,13},{9,17},{1... | collective-permute-start | bytes 786440 | tf_op jit(solution)/shard_map/kv1_1/ppermute | solution.py:123
  66.7 7.8 %collective-permute-start.18 = (bf16[256,512]{1,0:T(8,128)(2,1)S(1)}, bf16[256,512]{1,0:T(8,128)(2,1)S(1)}, u32[]{:S(2)}, u32[]{:S(2)}) collective-permute-start(bf16[256,512]{1,0:T(8,128)(2,1)S(1)} %get-tuple-element.66), channel_id=1, source_target_pairs={{0,4},{4,0},{8,12},{12,8},{16,20},{20,16},{24,28},{28,24},{1,5},{5... | collective-permute-start | bytes 786440 | tf_op jit(solution)/shard_map/o0/ppermute | solution.py:89
  73.8 1.8 %collective-permute-start.21 = (bf16[256,512]{1,0:T(8,128)(2,1)S(1)}, bf16[256,512]{1,0:T(8,128)(2,1)S(1)}, u32[]{:S(2)}, u32[]{:S(2)}) collective-permute-start(bf16[256,512]{1,0:T(8,128)(2,1)S(1)} %get-tuple-element.68), channel_id=1, source_target_pairs={{0,4},{4,0},{8,12},{12,8},{16,20},{20,16},{24,28},{28,24},{1,5},{5... | collective-permute-start | bytes 786440 | tf_op jit(solution)/shard_map/o1/ppermute | solution.py:89
  (2 other events, 23.2 us)

commit v4 on v3

--- a/solution.py
+++ b/solution.py
@@ -20,17 +20,26 @@
     return pl.CostEstimate(flops=int(flops), bytes_accessed=1 << 20, transcendentals=0)
 
 
-def attend_kernel(head, at_ref, docs_ref, own_ref, other_ref, *refs):
-    kv_refs, out_ref, bias_ref = refs[:-2], refs[-2], refs[-1]
+def attend_kernel(head, turns, at_ref, docs_ref, own_ref, other_ref, *refs):
+    kv_refs, out_refs, bias_ref = refs[: -len(turns) - 1], refs[-len(turns) - 1 : -1], refs[-1]
     core = lax.rem(at_ref[0], CORES)
     block = own_ref.shape[0]
     tokens = kv_refs[0].shape[0]
     back = len(kv_refs) - 1
-    group = out_ref.shape[2] // HS
+    group = out_refs[0].shape[1] // HS
     width = (REACH + 1) * block
     factor = 1.4426950408889634 / np.sqrt(HS)
     first_key = (at_ref[0] // CORES - back) * tokens
-    for b in range(CORES):
+
+    def window(low, columns):
+        parts = []
+        for i, ref in enumerate(kv_refs):
+            lo, hi = max(low - i * tokens, 0), min(low + width - i * tokens, tokens)
+            if lo < hi:
+                parts.append(ref[lo:hi, columns])
+        return jnp.concatenate(parts, axis=0)
+
+    def attend_block(b, turn, out_ref):
         q_pos = back * tokens + b * block + lax.broadcasted_iota(jnp.int32, (block, 1), 0)
         start = jnp.full((block, 1), -(2**30), jnp.int32)
         prefix = -first_key
@@ -38,42 +47,48 @@
             start = jnp.where(q_pos >= prefix, prefix, start)
             prefix = prefix + docs_ref[d]
         k_pos = b * block + lax.broadcasted_iota(jnp.int32, (block, width), 1)
-        bias_ref[b] = jnp.where((k_pos >= start) & (k_pos <= q_pos), 0.0, MASKED)
-
-    def window(low, columns):
-        parts = []
-        for i, ref in enumerate(kv_refs):
-            lo, hi = max(low - i * tokens, 0), min(low + width - i * tokens, tokens)
-            if lo < hi:
-                parts.append(ref[lo:hi, columns])
-        return jnp.concatenate(parts, axis=0)
-
-    for b in range(CORES):
+        bias_ref[...] = jnp.where((k_pos >= start) & (k_pos <= q_pos), 0.0, MASKED)
         keys = window(b * block, pl.ds(0, HS))
         values = window(b * block, pl.ds(HS, HS))
         values = jnp.concatenate([values, jnp.ones_like(values)], axis=1)
         for g in range(group):
-            own = own_ref[:, pl.ds(pl.multiple_of(((head * CORES + core) * group + g) * HS, HS), HS)]
-            column = (head * group + g) * HS
-            query = jnp.where(core == b, own, other_ref[:, column : column + HS])
+            query = (other_ref if turn else own_ref)[:, g * HS : (g + 1) * HS]
             score = lax.dot_general(query, keys, (((1,), (1,)), ((), ())), preferred_element_type=jnp.float32)
-            score = score + bias_ref[b]
+            score = score + bias_ref[...]
             top = jnp.max(score, axis=-1, keepdims=True)
             weight = jnp.exp2((score - top) * factor)
             summed = jnp.dot(weight.astype(jnp.bfloat16), values, preferred_element_type=jnp.float32)
-            out_ref[core ^ b, :, g * HS : (g + 1) * HS] = (summed[:, :HS] / summed[:, HS:]).astype(jnp.bfloat16)
-
-
-def attend(head, heads, at, docs, own, other, kvs):
+            out_ref[:, g * HS : (g + 1) * HS] = (summed[:, :HS] / summed[:, HS:]).astype(jnp.bfloat16)
+
+    for turn, out_ref in zip(turns, out_refs):
+        for b in range(CORES):
+            pl.when((core ^ turn) == b)(functools.partial(attend_block, b, turn, out_ref))
+
+
+def attend(head, heads, turns, at, docs, own, other, kvs):
     block = own.shape[0]
+    share = other.shape[1] // heads
+
+    def whole(x):
+        return pl.BlockSpec(x.shape, lambda i, at: (0,) * x.ndim)
+
     return pl.pallas_call(
-        functools.partial(attend_kernel, head),
-        out_shape=jax.ShapeDtypeStruct((CORES, own.shape[0], other.shape[1] // heads), jnp.bfloat16),
-        in_specs=[SMEM] * 2 + [VMEM] * (2 + len(kvs)),
-        out_specs=VMEM,
-        scratch_shapes=[pltpu.VMEM((CORES, block, (REACH + 1) * block), jnp.float32)],
+        functools.partial(attend_kernel, head, turns),
+        out_shape=[jax.ShapeDtypeStruct((block, share), jnp.bfloat16)] * len(turns),
+        grid_spec=pltpu.PrefetchScalarGridSpec(
+            num_scalar_prefetch=1,
+            grid=(1,),
+            in_specs=[
+                SMEM,
+                pl.BlockSpec((block, share), lambda i, at: (0, head * CORES + lax.rem(at[0], CORES))),
+                pl.BlockSpec((block, share), lambda i, at: (0, head)),
+            ]
+            + [whole(x) for x in kvs],
+            out_specs=[pl.BlockSpec((block, share), lambda i, at: (0, 0))] * len(turns),
+            scratch_shapes=[pltpu.VMEM((block, (REACH + 1) * block), jnp.float32)],
+        ),
         compiler_params=pltpu.CompilerParams(vmem_limit_bytes=32 << 20),
-        cost_estimate=cost(5e9),
+        cost_estimate=cost(2.5e9 * len(turns)),
         name="attend",
     )(at, docs, own, other, *kvs)
 
@@ -105,9 +120,9 @@
 
     pieces = [slot[:, : CORES * HS]]
 
-    def over_dp(h, piece):
-        slots = [piece]
-        for k in range(1, n_dp):
+    def over_dp(h, piece, steps):
+        slots = []
+        for k in steps:
             with jax.named_scope(f"z{h}_{k}"):
                 slots.append(lax.ppermute(piece, "dp", [(i, i ^ k) for i in range(n_dp)]))
         return slots
@@ -122,7 +137,7 @@
         with jax.named_scope(name):
             return lax.ppermute(x, "ctx", [(i, i + by * CORES) for i in range(n_ctx - by * CORES)])
 
-    slots = over_dp(0, pieces[0])
+    slots = [pieces[0]] + over_dp(0, pieces[0], range(1, n_dp))
     xf = hidden_in[0].astype(jnp.float32)
     scaled = (
         xf
@@ -144,7 +159,7 @@
         mine, theirs = jnp.where(core == 0, low, high), jnp.where(core == 0, high, low)
         if h + 1 < heads:
             piece, theirs = lax.optimization_barrier((pieces[h + 1], theirs))
-            slots = over_dp(h + 1, piece)
+            slots = [piece] + over_dp(h + 1, piece, range(1, n_dp - 1))
         if h:
             q_all = after(queries[0], theirs)
             q_other = jnp.concatenate(
@@ -162,6 +177,7 @@
                 )
                 for o in range(chips)
             ]
+            slots += over_dp(h + 1, after(piece, parts[0]), range(n_dp - 1, n_dp))
             for o in range(CORES, n_ctx, CORES):
                 parts.append(exchange(parts[0], o, n_ctx, f"w{h}_{o}"))
                 order.append(o)
@@ -185,8 +201,13 @@
         own = queries[0]
         if h + 1 < heads:
             own = after(own, window[h + 1][-1])
-        out = attend(h, heads, at[None], doc_lengths[0], own, q_other, window[h])
-        outs.append(both_cores(core, out[0], exchange(out[1], 1, n_ctx, f"o{h}"), 1))
+        rest = (at[None], doc_lengths[0], own, q_other, window[h])
+        if h + 1 < heads:
+            theirs, mine = attend(h, heads, (1, 0), *rest)
+        else:
+            (theirs,) = attend(h, heads, (1,), *rest)
+            (mine,) = attend(h, heads, (0,), *rest[:3], after(q_other, theirs), rest[4])
+        outs.append(both_cores(core, mine, exchange(theirs, 1, n_ctx, f"o{h}"), 1))
     return jnp.concatenate(outs, axis=1)[None]
 
 

time: 78.3 us -> 78 us (level)
  starting transfers between devices: 34.2 us -> 30.2 us
  waiting for transfers between devices: 20.1 us -> 22.8 us
  Pallas kernels: 9.82 us -> 11.5 us
    ppermute x12, starting transfers between devices: 15.2 us -> 12.4 us  [exchange(): return lax.ppermute(x, 'ctx', [(i, i ^ bit) for i in range(size)])]
    pallas_call x2 -> x3, Pallas kernels: 9.82 us -> 11.5 us  [attend(): pl.pallas_call(functools.partial(attend_kernel, head, turns), out_shape=[...]
    ppermute x4, waiting for transfers between devices: 0.01 us -> 1.59 us  [forward(): lax.ppermute(x, 'ctx', [(i, i + by * CORES) for i in range(n_ctx - by * C...]
    ppermute x4, starting transfers between devices: 10.6 us -> 9.55 us  [forward(): lax.ppermute(x, 'ctx', [(i, i + by * CORES) for i in range(n_ctx - by * C...]
    ppermute x12, waiting for transfers between devices: 10.8 us -> 11.6 us  [exchange(): return lax.ppermute(x, 'ctx', [(i, i ^ bit) for i in range(size)])]
  transfers between devices with their start and end apart: 22 -> 22, of which waited for: 6 -> 8; matrix products, arithmetic and copies ran while one was open for 11% -> 11% of each run, Pallas kernels for 13% -> 15%
where the time goes in v4:
time: 78 us; the launch traced here: 76.9 us
  starting transfers between devices  30.2 us (39%)
  waiting for transfers between devices  22.8 us (29%)
  Pallas kernels  11.5 us (15%)
  other arithmetic  6.47 us (8%)
  matrix products  2.37 us (3%)
  local copies, waits for them, and re-layouts  1.96 us (3%)
  between operations  1.63 us (2%)
    ppermute x12, starting transfers between devices, exchange(): return lax.ppermute(x, 'ctx', [(i, i ^ bit) for i in range(size)])  12.4 us
    ppermute x12, waiting for transfers between devices, exchange(): return lax.ppermute(x, 'ctx', [(i, i ^ bit) for i in range(size)])  11.6 us
    pallas_call x3, Pallas kernels, attend(): pl.pallas_call(functools.partial(attend_kernel, head, turns), out_shape=[...  11.5 us
    ppermute x4, starting transfers between devices, forward(): lax.ppermute(x, 'ctx', [(i, i + by * CORES) for i in range(n_ctx - by * C...  9.55 us
    ppermute x6, waiting for transfers between devices, over_dp(): slots.append(lax.ppermute(piece, 'dp', [(i, i ^ k) for i in range(n_dp)]))  9.54 us
    ppermute x6, starting transfers between devices, over_dp(): slots.append(lax.ppermute(piece, 'dp', [(i, i ^ k) for i in range(n_dp)]))  8.25 us
    dot_general x8, matrix products, local(): jnp.dot(columns[o // CORES], part, preferred_element_type=jnp.float32)  2.37 us
    ppermute x4, waiting for transfers between devices, forward(): lax.ppermute(x, 'ctx', [(i, i + by * CORES) for i in range(n_ctx - by * C...  1.59 us
  transfers between devices with their start and end apart: 22, of which 8 were waited for; matrix products, arithmetic and copies ran while one was open for 11% of the time, Pallas kernels for 15%

profile of v4, /device:TPU:1, one launch (start us, length us, event | category | flops | bytes accessed | tf_op | source)
XLA Modules:
  0.0 76.9 jit_solution(16491897851266846729)
XLA Ops:
  1.0 4.2 %collective-permute-start.2 = (bf16[256,256]{1,0:T(8,128)(2,1)S(1)}, bf16[256,256]{1,0:T(8,128)(2,1)S(1)}, u32[]{:S(2)}, u32[]{:S(2)}) collective-permute-start(bf16[256,256]{1,0:T(8,128)(2,1)S(1)} %slice.50), channel_id=1, source_target_pairs={{0,3},{1,2},{2,1},{3,0},{4,7},{5,6},{6,5},{7,4},{8,11},{9,10},{10,... | collective-permute-start | bytes 393224 | tf_op jit(solution)/shard_map/z0_3/ppermute | solution.py:127
  5.6 1.5 %fusion = f32[256]{0:T(256)S(1)} fusion(bf16[1,256,2048]{2,1,0:T(8,128)(2,1)} %param.6), kind=kLoop, calls=%fused_computation.2 | loop fusion | flops 1572608 | bytes 1049600 | tf_op jit(solution)/shard_map/reduce_sum | solution.py:144
  7.8 1.5 %fusion.2 = bf16[256,2048]{1,0:T(8,128)(2,1)S(1)} fusion(bf16[1,256,2048]{2,1,0:T(8,128)(2,1)} %param.6, f32[2048]{0:T(1024)S(1)} %convert_element_type.20, f32[256]{0:T(256)S(1)} %add_rsqrt_fusion), kind=kLoop, calls=%fused_computation.4 | loop fusion | flops 2097152 | bytes 2106368 | tf_op jit(solution)/shard_map/convert_element_type | solution.py:146
  9.3 6.5 %collective-permute-done.1 = bf16[256,256]{1,0:T(8,128)(2,1)S(1)} collective-permute-done((bf16[256,256]{1,0:T(8,128)(2,1)S(1)}, bf16[256,256]{1,0:T(8,128)(2,1)S(1)}, u32[]{:S(2)}, u32[]{:S(2)}) %collective-permute-start.1) | collective-permute-done | bytes 131104 | tf_op jit(solution)/shard_map/z0_2/ppermute | solution.py:127
  15.9 1.4 %collective-permute-start.6 = (bf16[256,2048]{1,0:T(8,128)(2,1)S(1)}, bf16[256,2048]{1,0:T(8,128)(2,1)S(1)}, u32[]{:S(2)}, u32[]{:S(2)}) collective-permute-start(bf16[256,2048]{1,0:T(8,128)(2,1)S(1)} %fusion.2), channel_id=1, source_target_pairs={{0,4},{4,0},{8,12},{12,8},{16,20},{20,16},{24,28},{28,24},{1,5},{5... | collective-permute-start | bytes 3145736 | tf_op jit(solution)/shard_map/s/ppermute | solution.py:104
  19.4 2.5 %collective-permute-start.3 = (bf16[256,256]{1,0:T(8,128)(2,1)S(1)}, bf16[256,256]{1,0:T(8,128)(2,1)S(1)}, u32[]{:S(2)}, u32[]{:S(2)}) collective-permute-start(bf16[256,256]{1,0:T(8,128)(2,1)S(1)} %slice.39), channel_id=1, source_target_pairs={{0,1},{1,0},{2,3},{3,2},{4,5},{5,4},{6,7},{7,6},{8,9},{9,8},{10,11... | collective-permute-start | bytes 393224 | tf_op jit(solution)/shard_map/z1_1/ppermute | solution.py:127
  21.9 2.2 %collective-permute-start.15 = (bf16[512,256]{1,0:T(8,128)(2,1)S(1)}, bf16[512,256]{1,0:T(8,128)(2,1)S(1)}, u32[]{:S(2)}, u32[]{:S(2)}) collective-permute-start(bf16[512,256]{1,0:T(8,128)(2,1)S(1)} %pad_maximum_fusion.5), channel_id=1, source_target_pairs={{0,24},{4,28},{8,16},{12,20},{16,8},{20,12},{24,0},{28,4},{1,25},{... | collective-permute-start | bytes 786440 | tf_op jit(solution)/shard_map/w0_6/ppermute | solution.py:104
  25.4 1.1 %collective-permute-start.7 = (bf16[256,256]{1,0:T(8,128)(2,1)S(1)}, bf16[256,256]{1,0:T(8,128)(2,1)S(1)}, u32[]{:S(2)}, u32[]{:S(2)}) collective-permute-start(bf16[256,256]{1,0:T(8,128)(2,1)S(1)} %slice.39), channel_id=1, source_target_pairs={{0,3},{1,2},{2,1},{3,0},{4,7},{5,6},{6,5},{7,4},{8,11},{9,10},{10,... | collective-permute-start | bytes 393224 | tf_op jit(solution)/shard_map/z1_3/ppermute | solution.py:127
  27.0 1.5 %collective-permute-done.4 = bf16[256,256]{1,0:T(8,128)(2,1)S(1)} collective-permute-done((bf16[256,256]{1,0:T(8,128)(2,1)S(1)}, bf16[256,256]{1,0:T(8,128)(2,1)S(1)}, u32[]{:S(2)}, u32[]{:S(2)}) %collective-permute-start.4) | collective-permute-done | bytes 131104 | tf_op jit(solution)/shard_map/z1_2/ppermute | solution.py:127
  28.4 1.2 %collective-permute-start.13 = (bf16[512,256]{1,0:T(8,128)(2,1)S(1)}, bf16[512,256]{1,0:T(8,128)(2,1)S(1)}, u32[]{:S(2)}, u32[]{:S(2)}) collective-permute-start(bf16[512,256]{1,0:T(8,128)(2,1)S(1)} %pad_maximum_fusion.5), channel_id=1, source_target_pairs={{0,8},{4,12},{8,0},{12,4},{16,24},{20,28},{24,16},{28,20},{1,9},{5... | collective-permute-start | bytes 786440 | tf_op jit(solution)/shard_map/w0_2/ppermute | solution.py:104
  29.7 1.5 %collective-permute-done.7 = bf16[256,256]{1,0:T(8,128)(2,1)S(1)} collective-permute-done((bf16[256,256]{1,0:T(8,128)(2,1)S(1)}, bf16[256,256]{1,0:T(8,128)(2,1)S(1)}, u32[]{:S(2)}, u32[]{:S(2)}) %collective-permute-start.7) | collective-permute-done | bytes 131104 | tf_op jit(solution)/shard_map/z1_3/ppermute | solution.py:127
  31.3 2.7 %collective-permute-start.8 = (bf16[256,256]{1,0:T(8,128)(2,1)S(1)}, bf16[256,256]{1,0:T(8,128)(2,1)S(1)}, u32[]{:S(2)}, u32[]{:S(2)}) collective-permute-start(bf16[256,256]{1,0:T(8,128)(2,1)S(1)} %get-tuple-element.78), channel_id=1, source_target_pairs={{0,4},{4,0},{8,12},{12,8},{16,20},{20,16},{24,28},{28,24},{1,5},{5... | collective-permute-start | bytes 393224 | tf_op jit(solution)/shard_map/c1/ppermute | solution.py:104
  35.0 1.3 %collective-permute-start.9 = (bf16[512,256]{1,0:T(8,128)(2,1)S(1)}, bf16[512,256]{1,0:T(8,128)(2,1)S(1)}, u32[]{:S(2)}, u32[]{:S(2)}) collective-permute-start(bf16[512,256]{1,0:T(8,128)(2,1)S(1)} %pad_maximum_fusion.6), channel_id=1, source_target_pairs={{0,16},{4,20},{8,24},{12,28},{16,0},{20,4},{24,8},{28,12},{1,17},{... | collective-permute-start | bytes 786440 | tf_op jit(solution)/shard_map/w1_4_0/ppermute | solution.py:104
  38.0 3.1 %collective-permute-start.17 = (bf16[512,256]{1,0:T(8,128)(2,1)S(1)}, bf16[512,256]{1,0:T(8,128)(2,1)S(1)}, u32[]{:S(2)}, u32[]{:S(2)}) collective-permute-start(bf16[512,256]{1,0:T(8,128)(2,1)S(1)} %fusion.8.refs_2_), channel_id=1, source_target_pairs={{0,8},{4,12},{8,16},{12,20},{16,24},{20,28},{1,9},{5,13},{9,17},{1... | collective-permute-start | bytes 786440 | tf_op jit(solution)/shard_map/kv0_1/ppermute | solution.py:138
  41.1 2.2 %collective-permute-start.16 = (bf16[512,256]{1,0:T(8,128)(2,1)S(1)}, bf16[512,256]{1,0:T(8,128)(2,1)S(1)}, u32[]{:S(2)}, u32[]{:S(2)}) collective-permute-start(bf16[512,256]{1,0:T(8,128)(2,1)S(1)} %fusion.8.refs_2_), channel_id=1, source_target_pairs={{0,16},{4,20},{8,24},{12,28},{1,17},{5,21},{9,25},{13,29},{2,18},{... | collective-permute-start | bytes 786440 | tf_op jit(solution)/shard_map/kv0_2/ppermute | solution.py:138
  44.4 10.4 %collective-permute-done.11 = bf16[512,256]{1,0:T(8,128)(2,1)S(1)} collective-permute-done((bf16[512,256]{1,0:T(8,128)(2,1)S(1)}, bf16[512,256]{1,0:T(8,128)(2,1)S(1)}, u32[]{:S(2)}, u32[]{:S(2)}) %collective-permute-start.11) | collective-permute-done | bytes 262176 | tf_op jit(solution)/shard_map/w1_2_1/ppermute | solution.py:104
  55.4 2.1 %collective-permute-start.20 = (bf16[512,256]{1,0:T(8,128)(2,1)S(1)}, bf16[512,256]{1,0:T(8,128)(2,1)S(1)}, u32[]{:S(2)}, u32[]{:S(2)}) collective-permute-start(bf16[512,256]{1,0:T(8,128)(2,1)S(1)} %fusion.7.refs_2_), channel_id=1, source_target_pairs={{0,8},{4,12},{8,16},{12,20},{16,24},{20,28},{1,9},{5,13},{9,17},{1... | collective-permute-start | bytes 786440 | tf_op jit(solution)/shard_map/kv1_1/ppermute | solution.py:138
  57.6 2.1 %collective-permute-start.19 = (bf16[512,256]{1,0:T(8,128)(2,1)S(1)}, bf16[512,256]{1,0:T(8,128)(2,1)S(1)}, u32[]{:S(2)}, u32[]{:S(2)}) collective-permute-start(bf16[512,256]{1,0:T(8,128)(2,1)S(1)} %fusion.7.refs_2_), channel_id=1, source_target_pairs={{0,16},{4,20},{8,24},{12,28},{1,17},{5,21},{9,25},{13,29},{2,18},{... | collective-permute-start | bytes 786440 | tf_op jit(solution)/shard_map/kv1_2/ppermute | solution.py:138
  59.8 5.4 %attend.3 = (bf16[256,512]{1,0:T(8,128)(2,1)S(1)}, bf16[256,512]{1,0:T(8,128)(2,1)S(1)}) custom-call(s32[1]{0:T(128)} %bitcast.at_ref, s32[4]{0:T(128)S(1)} %bitcast.31, bf16[256,2048]{1,0:T(8,128)(2,1)S(1)} %bitcast.28, bf16[256,1024]{1,0:T(8,128)(2,1)S(1)} %collective-permute-done.12.other_ref, bf16[512,256]{1,0:T(8,128)(2,1)S(1)} %collective-permute-done.16.refs_0_, ...), custom_call_target="tpu_custom_call" | custom-call | flops 5000000000 | bytes 1048576 | tf_op jit(solution)/shard_map/attend/pallas_call | solution.py:75
  65.2 2.1 %collective-permute-start.18 = (bf16[256,512]{1,0:T(8,128)(2,1)S(1)}, bf16[256,512]{1,0:T(8,128)(2,1)S(1)}, u32[]{:S(2)}, u32[]{:S(2)}) collective-permute-start(bf16[256,512]{1,0:T(8,128)(2,1)S(1)} %get-tuple-element.61), channel_id=1, source_target_pairs={{0,4},{4,0},{8,12},{12,8},{16,20},{20,16},{24,28},{28,24},{1,5},{5... | collective-permute-start | bytes 786440 | tf_op jit(solution)/shard_map/o0/ppermute | solution.py:104
  67.3 1.6 %collective-permute-done.19.refs_0_ = bf16[512,256]{1,0:T(8,128)(2,1)S(1)} collective-permute-done((bf16[512,256]{1,0:T(8,128)(2,1)S(1)}, bf16[512,256]{1,0:T(8,128)(2,1)S(1)}, u32[]{:S(2)}, u32[]{:S(2)}) %collective-permute-start.19) | collective-permute-done | bytes 262176 | tf_op jit(solution)/shard_map/kv1_2/ppermute | solution.py:138
  68.9 2.9 %attend.4 = bf16[256,512]{1,0:T(8,128)(2,1)S(1)} custom-call(s32[1]{0:T(128)} %bitcast.at_ref, s32[4]{0:T(128)S(1)} %bitcast.32, bf16[256,2048]{1,0:T(8,128)(2,1)S(1)} %bitcast.29, bf16[256,1024]{1,0:T(8,128)(2,1)S(1)} %collective-permute-done.12.other_ref, bf16[512,256]{1,0:T(8,128)(2,1)S(1)} %collective-permute-done.19.refs_0_, ...), custom_call_target="tpu_custom_call" | custom-call | flops 2500000000 | bytes 1048576 | tf_op jit(solution)/shard_map/attend/pallas_call | solution.py:75
  72.5 3.1 %attend.5 = bf16[256,512]{1,0:T(8,128)(2,1)S(1)} custom-call(s32[1]{0:T(128)} %bitcast.at_ref, s32[4]{0:T(128)S(1)} %bitcast.33, bf16[256,2048]{1,0:T(8,128)(2,1)S(1)} %bitcast.30, bf16[256,1024]{1,0:T(8,128)(2,1)S(1)} %collective-permute-done.12.other_ref, bf16[512,256]{1,0:T(8,128)(2,1)S(1)} %collective-permute-done.19.refs_0_, ...), custom_call_target="tpu_custom_call" | custom-call | flops 2500000000 | bytes 1048576 | tf_op jit(solution)/shard_map/attend/pallas_call | solution.py:75
  75.8 1.0 %maximum_bitcast_fusion = bf16[1,256,2048]{2,1,0:T(8,128)(2,1)} fusion(bf16[256,1024]{1,0:T(8,128)(2,1)S(1)} %maximum_select_fusion.2, bf16[256,1024]{1,0:T(8,128)(2,1)S(1)} %maximum_select_fusion.1), kind=kLoop, calls=%fused_computation.14 | loop fusion | flops 2097152 | bytes 2097152 | tf_op jit(solution)/shard_map/broadcast_in_dim | solution.py:211
  (66 shorter events, 9.9 us)
Async XLA Ops:
  0.0 19.0 %copy-start.2 = (bf16[1,256,512]{2,1,0:T(8,128)(2,1)S(1)}, bf16[1,256,512]{2,1,0:T(8,128)(2,1)}, u32[]{:S(2)}) copy-start(bf16[1,256,512]{2,1,0:T(8,128)(2,1)} %param.9) | copy-start | bytes 786436
  0.0 17.2 %copy-start.3 = (s32[2]{0:T(128)S(1)}, s32[2]{0:T(128)}, u32[]{:S(2)}) copy-start(s32[2]{0:T(128)} %param.10) | copy-start | bytes 28
  1.0 8.3 %collective-permute-start.2 = (bf16[256,256]{1,0:T(8,128)(2,1)S(1)}, bf16[256,256]{1,0:T(8,128)(2,1)S(1)}, u32[]{:S(2)}, u32[]{:S(2)}) collective-permute-start(bf16[256,256]{1,0:T(8,128)(2,1)S(1)} %slice.50), channel_id=1, source_target_pairs={{0,3},{1,2},{2,1},{3,0},{4,7},{5,6},{6,5},{7,4},{8,11},{9,10},{10,... | collective-permute-start | bytes 393224 | tf_op jit(solution)/shard_map/z0_3/ppermute | solution.py:127
  5.2 10.7 %collective-permute-start.1 = (bf16[256,256]{1,0:T(8,128)(2,1)S(1)}, bf16[256,256]{1,0:T(8,128)(2,1)S(1)}, u32[]{:S(2)}, u32[]{:S(2)}) collective-permute-start(bf16[256,256]{1,0:T(8,128)(2,1)S(1)} %slice.50), channel_id=1, source_target_pairs={{0,2},{1,3},{2,0},{3,1},{4,6},{5,7},{6,4},{7,5},{8,10},{9,11},{10,... | collective-permute-start | bytes 393224 | tf_op jit(solution)/shard_map/z0_2/ppermute | solution.py:127
  5.2 10.7 %collective-permute-start = (bf16[256,256]{1,0:T(8,128)(2,1)S(1)}, bf16[256,256]{1,0:T(8,128)(2,1)S(1)}, u32[]{:S(2)}, u32[]{:S(2)}) collective-permute-start(bf16[256,256]{1,0:T(8,128)(2,1)S(1)} %slice.50), channel_id=1, source_target_pairs={{0,1},{1,0},{2,3},{3,2},{4,5},{5,4},{6,7},{7,6},{8,9},{9,8},{10,11... | collective-permute-start | bytes 393224 | tf_op jit(solution)/shard_map/z0_1/ppermute | solution.py:127
  15.9 6.0 %collective-permute-start.6 = (bf16[256,2048]{1,0:T(8,128)(2,1)S(1)}, bf16[256,2048]{1,0:T(8,128)(2,1)S(1)}, u32[]{:S(2)}, u32[]{:S(2)}) collective-permute-start(bf16[256,2048]{1,0:T(8,128)(2,1)S(1)} %fusion.2), channel_id=1, source_target_pairs={{0,4},{4,0},{8,12},{12,8},{16,20},{20,16},{24,28},{28,24},{1,5},{5... | collective-permute-start | bytes 3145736 | tf_op jit(solution)/shard_map/s/ppermute | solution.py:104
  19.2 2.7 %collective-permute-start.5 = (bf16[256,256]{1,0:T(8,128)(2,1)S(1)}, bf16[256,256]{1,0:T(8,128)(2,1)S(1)}, u32[]{:S(2)}, u32[]{:S(2)}) collective-permute-start(bf16[256,256]{1,0:T(8,128)(2,1)S(1)} %get-tuple-element.41), channel_id=1, source_target_pairs={{0,4},{4,0},{8,12},{12,8},{16,20},{20,16},{24,28},{28,24},{1,5},{5... | collective-permute-start | bytes 393224 | tf_op jit(solution)/shard_map/c0/ppermute | solution.py:104
  19.3 9.1 %collective-permute-start.4 = (bf16[256,256]{1,0:T(8,128)(2,1)S(1)}, bf16[256,256]{1,0:T(8,128)(2,1)S(1)}, u32[]{:S(2)}, u32[]{:S(2)}) collective-permute-start(bf16[256,256]{1,0:T(8,128)(2,1)S(1)} %slice.39), channel_id=1, source_target_pairs={{0,2},{1,3},{2,0},{3,1},{4,6},{5,7},{6,4},{7,5},{8,10},{9,11},{10,... | collective-permute-start | bytes 393224 | tf_op jit(solution)/shard_map/z1_2/ppermute | solution.py:127
  19.4 10.2 %collective-permute-start.3 = (bf16[256,256]{1,0:T(8,128)(2,1)S(1)}, bf16[256,256]{1,0:T(8,128)(2,1)S(1)}, u32[]{:S(2)}, u32[]{:S(2)}) collective-permute-start(bf16[256,256]{1,0:T(8,128)(2,1)S(1)} %slice.39), channel_id=1, source_target_pairs={{0,1},{1,0},{2,3},{3,2},{4,5},{5,4},{6,7},{7,6},{8,9},{9,8},{10,11... | collective-permute-start | bytes 393224 | tf_op jit(solution)/shard_map/z1_1/ppermute | solution.py:127
  21.9 14.4 %collective-permute-start.15 = (bf16[512,256]{1,0:T(8,128)(2,1)S(1)}, bf16[512,256]{1,0:T(8,128)(2,1)S(1)}, u32[]{:S(2)}, u32[]{:S(2)}) collective-permute-start(bf16[512,256]{1,0:T(8,128)(2,1)S(1)} %pad_maximum_fusion.5), channel_id=1, source_target_pairs={{0,24},{4,28},{8,16},{12,20},{16,8},{20,12},{24,0},{28,4},{1,25},{... | collective-permute-start | bytes 786440 | tf_op jit(solution)/shard_map/w0_6/ppermute | solution.py:104
  24.2 12.6 %collective-permute-start.14 = (bf16[512,256]{1,0:T(8,128)(2,1)S(1)}, bf16[512,256]{1,0:T(8,128)(2,1)S(1)}, u32[]{:S(2)}, u32[]{:S(2)}) collective-permute-start(bf16[512,256]{1,0:T(8,128)(2,1)S(1)} %pad_maximum_fusion.5), channel_id=1, source_target_pairs={{0,16},{4,20},{8,24},{12,28},{16,0},{20,4},{24,8},{28,12},{1,17},{... | collective-permute-start | bytes 786440 | tf_op jit(solution)/shard_map/w0_4/ppermute | solution.py:104
  25.4 5.8 %collective-permute-start.7 = (bf16[256,256]{1,0:T(8,128)(2,1)S(1)}, bf16[256,256]{1,0:T(8,128)(2,1)S(1)}, u32[]{:S(2)}, u32[]{:S(2)}) collective-permute-start(bf16[256,256]{1,0:T(8,128)(2,1)S(1)} %slice.39), channel_id=1, source_target_pairs={{0,3},{1,2},{2,1},{3,0},{4,7},{5,6},{6,5},{7,4},{8,11},{9,10},{10,... | collective-permute-start | bytes 393224 | tf_op jit(solution)/shard_map/z1_3/ppermute | solution.py:127
  28.4 8.3 %collective-permute-start.13 = (bf16[512,256]{1,0:T(8,128)(2,1)S(1)}, bf16[512,256]{1,0:T(8,128)(2,1)S(1)}, u32[]{:S(2)}, u32[]{:S(2)}) collective-permute-start(bf16[512,256]{1,0:T(8,128)(2,1)S(1)} %pad_maximum_fusion.5), channel_id=1, source_target_pairs={{0,8},{4,12},{8,0},{12,4},{16,24},{20,28},{24,16},{28,20},{1,9},{5... | collective-permute-start | bytes 786440 | tf_op jit(solution)/shard_map/w0_2/ppermute | solution.py:104
  31.3 3.7 %collective-permute-start.8 = (bf16[256,256]{1,0:T(8,128)(2,1)S(1)}, bf16[256,256]{1,0:T(8,128)(2,1)S(1)}, u32[]{:S(2)}, u32[]{:S(2)}) collective-permute-start(bf16[256,256]{1,0:T(8,128)(2,1)S(1)} %get-tuple-element.78), channel_id=1, source_target_pairs={{0,4},{4,0},{8,12},{12,8},{16,20},{20,16},{24,28},{28,24},{1,5},{5... | collective-permute-start | bytes 393224 | tf_op jit(solution)/shard_map/c1/ppermute | solution.py:104
  34.1 25.6 %collective-permute-start.12 = (bf16[256,1024]{1,0:T(8,128)(2,1)S(1)}, bf16[256,1024]{1,0:T(8,128)(2,1)S(1)}, u32[]{:S(2)}, u32[]{:S(2)}) collective-permute-start(bf16[256,1024]{1,0:T(8,128)(2,1)S(1)} %pad_maximum_fusion.4), channel_id=1, source_target_pairs={{0,4},{4,0},{8,12},{12,8},{16,20},{20,16},{24,28},{28,24},{1,5},{5... | collective-permute-start | bytes 1572872 | tf_op jit(solution)/shard_map/q/ppermute | solution.py:104
  35.0 8.2 %collective-permute-start.9 = (bf16[512,256]{1,0:T(8,128)(2,1)S(1)}, bf16[512,256]{1,0:T(8,128)(2,1)S(1)}, u32[]{:S(2)}, u32[]{:S(2)}) collective-permute-start(bf16[512,256]{1,0:T(8,128)(2,1)S(1)} %pad_maximum_fusion.6), channel_id=1, source_target_pairs={{0,16},{4,20},{8,24},{12,28},{16,0},{20,4},{24,8},{28,12},{1,17},{... | collective-permute-start | bytes 786440 | tf_op jit(solution)/shard_map/w1_4_0/ppermute | solution.py:104
  36.3 7.2 %collective-permute-start.10 = (bf16[512,256]{1,0:T(8,128)(2,1)S(1)}, bf16[512,256]{1,0:T(8,128)(2,1)S(1)}, u32[]{:S(2)}, u32[]{:S(2)}) collective-permute-start(bf16[512,256]{1,0:T(8,128)(2,1)S(1)} %pad_maximum_fusion.6), channel_id=1, source_target_pairs={{0,8},{4,12},{8,0},{12,4},{16,24},{20,28},{24,16},{28,20},{1,9},{5... | collective-permute-start | bytes 786440 | tf_op jit(solution)/shard_map/w1_2_0/ppermute | solution.py:104
  38.0 21.8 %collective-permute-start.17 = (bf16[512,256]{1,0:T(8,128)(2,1)S(1)}, bf16[512,256]{1,0:T(8,128)(2,1)S(1)}, u32[]{:S(2)}, u32[]{:S(2)}) collective-permute-start(bf16[512,256]{1,0:T(8,128)(2,1)S(1)} %fusion.8.refs_2_), channel_id=1, source_target_pairs={{0,8},{4,12},{8,16},{12,20},{16,24},{20,28},{1,9},{5,13},{9,17},{1... | collective-permute-start | bytes 786440 | tf_op jit(solution)/shard_map/kv0_1/ppermute | solution.py:138
  41.1 18.6 %collective-permute-start.16 = (bf16[512,256]{1,0:T(8,128)(2,1)S(1)}, bf16[512,256]{1,0:T(8,128)(2,1)S(1)}, u32[]{:S(2)}, u32[]{:S(2)}) collective-permute-start(bf16[512,256]{1,0:T(8,128)(2,1)S(1)} %fusion.8.refs_2_), channel_id=1, source_target_pairs={{0,16},{4,20},{8,24},{12,28},{1,17},{5,21},{9,25},{13,29},{2,18},{... | collective-permute-start | bytes 786440 | tf_op jit(solution)/shard_map/kv0_2/ppermute | solution.py:138
  43.6 11.3 %collective-permute-start.11 = (bf16[512,256]{1,0:T(8,128)(2,1)S(1)}, bf16[512,256]{1,0:T(8,128)(2,1)S(1)}, u32[]{:S(2)}, u32[]{:S(2)}) collective-permute-start(bf16[512,256]{1,0:T(8,128)(2,1)S(1)} %collective-permute-done.9), channel_id=1, source_target_pairs={{0,8},{4,12},{8,0},{12,4},{16,24},{20,28},{24,16},{28,20},{1,9},{5... | collective-permute-start | bytes 786440 | tf_op jit(solution)/shard_map/w1_2_1/ppermute | solution.py:104
  55.4 11.9 %collective-permute-start.20 = (bf16[512,256]{1,0:T(8,128)(2,1)S(1)}, bf16[512,256]{1,0:T(8,128)(2,1)S(1)}, u32[]{:S(2)}, u32[]{:S(2)}) collective-permute-start(bf16[512,256]{1,0:T(8,128)(2,1)S(1)} %fusion.7.refs_2_), channel_id=1, source_target_pairs={{0,8},{4,12},{8,16},{12,20},{16,24},{20,28},{1,9},{5,13},{9,17},{1... | collective-permute-start | bytes 786440 | tf_op jit(solution)/shard_map/kv1_1/ppermute | solution.py:138
  57.6 11.3 %collective-permute-start.19 = (bf16[512,256]{1,0:T(8,128)(2,1)S(1)}, bf16[512,256]{1,0:T(8,128)(2,1)S(1)}, u32[]{:S(2)}, u32[]{:S(2)}) collective-permute-start(bf16[512,256]{1,0:T(8,128)(2,1)S(1)} %fusion.7.refs_2_), channel_id=1, source_target_pairs={{0,16},{4,20},{8,24},{12,28},{1,17},{5,21},{9,25},{13,29},{2,18},{... | collective-permute-start | bytes 786440 | tf_op jit(solution)/shard_map/kv1_2/ppermute | solution.py:138
  65.2 7.2 %collective-permute-start.18 = (bf16[256,512]{1,0:T(8,128)(2,1)S(1)}, bf16[256,512]{1,0:T(8,128)(2,1)S(1)}, u32[]{:S(2)}, u32[]{:S(2)}) collective-permute-start(bf16[256,512]{1,0:T(8,128)(2,1)S(1)} %get-tuple-element.61), channel_id=1, source_target_pairs={{0,4},{4,0},{8,12},{12,8},{16,20},{20,16},{24,28},{28,24},{1,5},{5... | collective-permute-start | bytes 786440 | tf_op jit(solution)/shard_map/o0/ppermute | solution.py:104
  71.8 3.8 %collective-permute-start.21 = (bf16[256,512]{1,0:T(8,128)(2,1)S(1)}, bf16[256,512]{1,0:T(8,128)(2,1)S(1)}, u32[]{:S(2)}, u32[]{:S(2)}) collective-permute-start(bf16[256,512]{1,0:T(8,128)(2,1)S(1)} %attend.4), channel_id=1, source_target_pairs={{0,4},{4,0},{8,12},{12,8},{16,20},{20,16},{24,28},{28,24},{1,5},{5... | collective-permute-start | bytes 786440 | tf_op jit(solution)/shard_map/o1/ppermute | solution.py:104
  (2 other events, 22.5 us)
